TPU v7x, 1024 devices: a whole 4x4x32 slice. The times are simulated.
1024 devices in a mesh: seq: 32 (over z), head: 4 (over x), exp: 8 (over y, core).
Axes of the slice: x: 4, y: 4, z: 32, core: 2. Of those that a mesh axis runs over, the one named last changes fastest.
Arguments:
- x_in: bfloat16 [32768, 4096], P(('seq', 'exp'), 'head'), may hold values from -6 to 6
- z_in: bfloat16 [32768, 4096], P(('seq', 'exp'), 'head'), may hold values from -6 to 6
- b_in: bfloat16 [32768, 1024], P(('seq', 'exp'), 'head'), may hold values from -1.796875 to 1.796875
- c_in: bfloat16 [32768, 1024], P(('seq', 'exp'), 'head'), may hold values from -1.796875 to 1.796875
- dt_in: float32 [32768, 64], P(('seq', 'exp'), 'head'), may hold values from -5.4 to -1.7
- a_log: float32 [64], P('head'), may hold values from -12 to 2
- d_skip: float32 [64], P('head'), may hold values from 0.5 to 2
- norm_w: float32 [4096], P('head'), may hold values from 0.5 to 1.5
- w_out: bfloat16 [4096, 1344], P('head'), may hold values from -0.09375 to 0.09375
- resid: bfloat16 [256, 128, 1344], P(('seq', 'exp'), 'head'), may hold values from -30 to 30
- routes: int32 [256, 128, 6], P(('seq', 'exp'), 'head'), may hold values from 0 to 31, all different within a row; in each aligned block of 32 rows (0 to 31, 32 to 63, ..., all dimensions but the last counted through in order) at most 16 rows name the same one
- gates: float32 [256, 128, 6], P(('seq', 'exp'), 'head'), may hold values from 0.1 to 0.7
- moe_gain: float32 [1344], replicated, may hold values from 0.5 to 1.5
- w_up: bfloat16 [32, 1344, 928], P(('head', 'exp')), may hold values from -0.15625 to 0.15625
- w_down: bfloat16 [32, 928, 1344], P(('head', 'exp')), may hold values from -0.1875 to 0.1875
Outputs:
- output: bfloat16 [256, 128, 1344], P(('seq', 'exp'), 'head')
Inputs may be any that keep to these rules, and one draw needn't show every extreme that they name: `routes`: within the 32 aligned rows of one device no expert is named more than 16 times, and in every draw some expert is named exactly 16 times within some device's rows.
All inputs are finite; a program needn't handle non-finite values.
Results may differ from a plain program's by a relative error of at most 0.018.
Values may be sent and summed in bfloat16 or wider, within the bound.
A program may use at most 64 MiB of HBM per device.

v0:
```python
import math

import jax
import jax.numpy as jnp
from jax import lax
from jax.sharding import PartitionSpec as P

HEAD_DIM = 64
STATE = 128
STRETCH = 128


def side_by_side(arrays, axis, dim, along):
    widths = [math.prod(a.shape[along:]) for a in arrays]
    both = jnp.concatenate(
        [a.reshape(*a.shape[:along], w) for a, w in zip(arrays, widths)], axis=along
    )
    filled = lax.all_gather(both, axis, axis=dim, tiled=True)
    tiles = jnp.split(filled, [sum(widths[:k]) for k in range(1, len(widths))], axis=along)
    return tuple(
        (b.reshape(*filled.shape[:along], *a.shape[along:]) for a, b in zip(arrays, tiles))
    )


def prefix(shard, axis, combine, identity):
    count, index = (lax.axis_size(axis), lax.axis_index(axis))
    everything = jax.tree.map(
        lambda part, kind: lax.all_gather(part.astype(kind), axis),
        shard,
        (jnp.bfloat16, jnp.bfloat16),
    )
    start = jax.tree.map(
        lambda part, zero: jnp.broadcast_to(jnp.asarray(zero, part.dtype), part.shape),
        shard,
        identity,
    )

    def turn(k, before):
        reached = k < index
        new = combine(
            before, jax.tree.map(lambda part, own: part[k].astype(own.dtype), everything, shard)
        )
        return jax.tree.map(lambda a, b: jnp.where(reached, a, b), new, before)

    return lax.fori_loop(0, count, turn, start)


def cut_along(shard, dim, count):
    dims = shard.shape
    tiles = shard.reshape(*dims[:dim], count, dims[dim] // count, *dims[dim + 1 :])
    return jnp.moveaxis(tiles, dim, 0)


def sent_and_summed(shard, axis, dim):
    tiles = cut_along(shard, dim, lax.axis_size(axis))
    arrived = lax.all_to_all(tiles, axis, split_axis=0, concat_axis=0, tiled=True)
    return arrived.astype(jnp.float32).sum(axis=0)


def stretch_pass(carry_state, pieces):
    x_part, b_part, c_part, rate_part, step_part = pieces
    per_group = x_part.shape[1] // b_part.shape[1]
    b_heads = jnp.repeat(b_part, per_group, axis=1)
    c_heads = jnp.repeat(c_part, per_group, axis=1)
    cumulative = jnp.cumsum(rate_part, axis=0)
    cum_heads = cumulative.T
    distance = cum_heads[:, :, None] - cum_heads[:, None, :]
    length = cumulative.shape[0]
    causal = (jnp.arange(length)[:, None] >= jnp.arange(length)[None, :])[None]
    decay_mat = jnp.where(causal, jnp.exp(jnp.where(causal, distance, 0.0)), 0.0)
    weighting = decay_mat * step_part.T[:, None, :]
    scores = jnp.einsum("thn,shn->hts", c_heads, b_heads, preferred_element_type=jnp.float32)
    mixing = (scores * weighting).astype(jnp.bfloat16)
    inside = jnp.einsum("hts,shp->thp", mixing, x_part, preferred_element_type=jnp.float32)
    state_low = carry_state.astype(jnp.bfloat16)
    carried = jnp.exp(cumulative)[:, :, None] * jnp.einsum(
        "thn,hpn->thp", c_heads, state_low, preferred_element_type=jnp.float32
    )
    tail_weight = jnp.exp(cumulative[-1][None, :] - cumulative) * step_part
    weighted_x = (tail_weight[:, :, None] * x_part.astype(jnp.float32)).astype(jnp.bfloat16)
    update = jnp.einsum("shp,shn->hpn", weighted_x, b_heads, preferred_element_type=jnp.float32)
    new_state = jnp.exp(cumulative[-1])[:, None, None] * carry_state + update
    return (new_state, inside + carried)


def by_stretch(values):
    return values.reshape((values.shape[0] // STRETCH, STRETCH) + values.shape[1:])


def join_pairs(earlier, later):
    return (earlier[0] + later[0], jnp.exp(later[0])[:, None, None] * earlier[1] + later[1])


def expert_rows(row_block, w_up, w_down):
    model_width = row_block.shape[-1]
    flat_rows = row_block.reshape(-1, model_width)
    up_proj = jnp.dot(flat_rows, w_up[0], preferred_element_type=jnp.float32)
    activated = jnp.square(jnp.maximum(up_proj, 0.0)).astype(jnp.bfloat16)
    produced = jnp.dot(activated, w_down[0], preferred_element_type=jnp.float32).astype(
        jnp.bfloat16
    )
    return produced.reshape(row_block.shape)


def per_device(
    x_in,
    z_in,
    b_in,
    c_in,
    dt_in,
    a_log,
    d_skip,
    norm_w,
    w_out,
    resid,
    routes,
    gates,
    moe_gain,
    w_up,
    w_down,
):
    length, head_count = dt_in.shape
    groups = b_in.shape[1] // STATE
    per_group = head_count // groups
    low_values = x_in.reshape(length, head_count, HEAD_DIM)
    b_groups = b_in.reshape(length, groups, STATE)
    c_groups = c_in.reshape(length, groups, STATE)
    step_size = jax.nn.softplus(dt_in)
    log_rate = -step_size * jnp.exp(a_log)[None, :]
    zero_state = jnp.zeros((head_count, HEAD_DIM, STATE), jnp.float32)
    zero_decay = jnp.zeros((head_count,), jnp.float32)
    last_state, local_out = lax.scan(
        stretch_pass,
        zero_state,
        (
            by_stretch(low_values),
            by_stretch(b_groups),
            by_stretch(c_groups),
            by_stretch(log_rate),
            by_stretch(step_size),
        ),
    )
    local_out = local_out.reshape(length, head_count, HEAD_DIM)
    decay_sum = jnp.sum(log_rate, axis=0)
    group_decays, group_states = tuple(
        (
            part.astype(jnp.float32)
            for part in side_by_side(
                (decay_sum[None].astype(jnp.bfloat16), last_state[None].astype(jnp.bfloat16)),
                "exp",
                0,
                2,
            )
        )
    )

    def walk(carry_pair, item_pair):
        return (join_pairs(carry_pair, item_pair), carry_pair)

    span_pair, prefixes = lax.scan(walk, (zero_decay, zero_state), (group_decays, group_states))
    my_index = lax.axis_index("exp")
    inside_pair = (
        lax.dynamic_index_in_dim(prefixes[0], my_index, 0, keepdims=False),
        lax.dynamic_index_in_dim(prefixes[1], my_index, 0, keepdims=False),
    )
    chain_in = prefix((span_pair[0], span_pair[1]), "seq", join_pairs, (zero_decay, zero_state))
    before = join_pairs(chain_in, inside_pair)
    cum_device = jnp.cumsum(log_rate, axis=0)
    c_heads = jnp.repeat(c_groups, per_group, axis=1)
    before_low = before[1].astype(jnp.bfloat16)
    carried = jnp.exp(cum_device)[:, :, None] * jnp.einsum(
        "thn,hpn->thp", c_heads, before_low, preferred_element_type=jnp.float32
    )
    ssm_out = local_out + carried + d_skip[None, :, None] * low_values.astype(jnp.float32)
    gated_out = ssm_out * jax.nn.silu(
        z_in.astype(jnp.float32).reshape(length, head_count, HEAD_DIM)
    )
    grouped = gated_out.reshape(length, groups, -1)
    inverse = lax.rsqrt(jnp.mean(grouped * grouped, axis=2, keepdims=True) + 1e-05)
    normed = ((grouped * inverse).reshape(length, head_count * HEAD_DIM) * norm_w[None, :]).astype(
        jnp.bfloat16
    )
    rows_here = resid.shape[1]
    mixed = sent_and_summed(
        jnp.dot(normed, w_out, preferred_element_type=jnp.float32).astype(jnp.bfloat16), "head", 0
    )
    hidden = (resid[0].astype(jnp.float32) + mixed).astype(jnp.bfloat16)
    hidden_f32 = hidden.astype(jnp.float32)
    norm_scale = lax.rsqrt(jnp.mean(hidden_f32 * hidden_f32, axis=1, keepdims=True) + 1e-05)
    moe_in = (hidden_f32 * norm_scale * moe_gain[None, :]).astype(jnp.bfloat16)
    head_size = lax.axis_size("head")
    exp_size = lax.axis_size("exp")
    experts_all = head_size * exp_size
    picks = routes.shape[2]
    room = min(rows_here, 8 * ((2 * rows_here * picks // experts_all + 7) // 8))
    flat_routes = routes[0].reshape(-1)
    onehot = (flat_routes[:, None] == jnp.arange(experts_all, dtype=jnp.int32)[None, :]).astype(
        jnp.int32
    )
    position = jnp.sum((jnp.cumsum(onehot, axis=0) - onehot) * onehot, axis=1)
    slot_id = flat_routes * room + position
    slot_table = (
        slot_id[:, None] == jnp.arange(experts_all * room, dtype=jnp.int32)[None, :]
    ).reshape(rows_here, picks, experts_all * room)
    chosen = jnp.sum(slot_table.astype(jnp.bfloat16), axis=1)
    outbound = lax.dot_general(
        chosen, moe_in, (((0,), (0,)), ((), ())), preferred_element_type=jnp.float32
    )
    outbound = outbound.astype(jnp.bfloat16).reshape(experts_all, room, moe_in.shape[1])
    produced = expert_rows(
        lax.all_to_all(outbound, ("head", "exp"), split_axis=0, concat_axis=0, tiled=True),
        w_up,
        w_down,
    )
    returned = lax.all_to_all(produced, ("head", "exp"), split_axis=0, concat_axis=0, tiled=True)
    returned_flat = returned.reshape(experts_all * room, moe_in.shape[1])
    picked_rows = returned_flat[slot_id.reshape(rows_here, picks)]
    moe_sum = jnp.sum(picked_rows.astype(jnp.float32) * gates[0][:, :, None], axis=1)
    return (hidden_f32 + moe_sum).astype(jnp.bfloat16)[None]


def solution(mesh):
    placed = (
        P(("seq", "exp"), "head"),
        P(("seq", "exp"), "head"),
        P(("seq", "exp"), "head"),
        P(("seq", "exp"), "head"),
        P(("seq", "exp"), "head"),
        P("head"),
        P("head"),
        P("head"),
        P("head", None),
        P(("seq", "exp"), "head", None),
        P(("seq", "exp"), "head", None),
        P(("seq", "exp"), "head", None),
        P(),
        P(("head", "exp"), None, None),
        P(("head", "exp"), None, None),
    )
    return jax.shard_map(
        per_device,
        mesh=mesh,
        in_specs=placed,
        out_specs=P(("seq", "exp"), "head", None),
        check_vma=False,
    )
```

profile of v0, /device:TPU:1, one launch (start us, length us, event | category | flops | bytes accessed | tf_op | source)
XLA Modules:
  0.0 421.0 jit_solution(3800123033272704383)
XLA Ops:
  10.6 1.3 fusion.56
  14.3 52.0 %all-gather.5.cloned.1.call-done = bf16[8,16,8193]{2,1,0:T(8,128)(2,1)} async-done(((bf16[1,16,8193]{2,1,0:T(8,128)(2,1)}), bf16[8,16,8193]{2,1,0:T(8,128)(2,1)}) %all-gather.5.cloned.1.call-update) | async-done | bytes 2097424 | tf_op jit(solution)/shard_map/all_gather | solution.py:18
  66.3 2.3 slice_convert_fusion
  68.6 2.7 copy.136
  71.4 16.8 %while.36 = (s32[]{:T(128)}, f32[16]{0:T(128)S(1)}, f32[16,64,128]{2,1,0:T(8,128)S(1)}, f32[8,16]{1,0:T(8,128)S(1)}, f32[8,16,64,128]{3,2,1,0:T(8,128)}, /*index...) while((s32[]{:T(128)}, f32[16]{0:T(128)S(1)}, ...), condition=%wide.region_3.4_spmd.clone, body=%wide.region_2.3_spmd.clone.sunk | while | flops 524323 | bytes 2622581 | solution.py:160
  89.7 1.9 copy.120
  93.5 1.3 dynamic-slice.2
  97.0 1.3 fusion.17
  98.5 48.9 %all-reduce.1 = bf16[512]{0:T(512)(128)(2,1)S(1)} all-reduce(bf16[512]{0:T(512)(128)(2,1)S(1)} %dynamic-update-slice), channel_id=2, replica_groups=mesh['seq'=32,'head'=4,'exp'=8] {'seq'}, use_global_device_ids=true, to_apply=%add.1 | all-reduce | flops 512 | bytes 2048
  148.7 77.1 %all-gather.7.cloned.1.call-done = bf16[512,64,128]{2,1,0:T(8,128)(2,1)} async-done(((bf16[16,64,128]{2,1,0:T(8,128)(2,1)}), bf16[512,64,128]{2,1,0:T(8,128)(2,1)}) %all-gather.7.cloned.1.call-update) | async-done | bytes 8388624 | tf_op jit(solution)/shard_map/all_gather | solution.py:28
  225.8 75.3 %while.37 = (s32[]{:T(128)}, f32[16,64,128]{2,1,0:T(8,128)S(1)}, s32[]{:T(128)}, bf16[32,16]{1,0:T(8,128)(2,1)}, bf16[32,16,64,128]{3,2,1,0:T(8,128)(2,1)}, /*index=5*/s32[]{:T(128)}, s32[]{:T(128)}) while((s32[]{:T(128)}, f32[16,64,128]{2,1,0:T(8,128)S(1)}, s32[]{:T(128)}, bf16[32,16]{1,0:T(8,128)(2,1)}, ...), condition=%wide.region_5.6_spmd.clone, body=%wide.region_4.5_spmd.clone.sunk | while | flops 655380 | bytes 1310985 | solution.py:45
  225.8 1.3 exponential_bitcast_fusion.3
  228.2 1.3 exponential_bitcast_fusion.3
  230.6 1.3 exponential_bitcast_fusion.3
  233.0 1.3 exponential_bitcast_fusion.3
  235.4 1.3 exponential_bitcast_fusion.3
  237.8 1.3 exponential_bitcast_fusion.3
  240.1 1.3 exponential_bitcast_fusion.3
  242.5 1.3 exponential_bitcast_fusion.3
  263.5 1.3 exponential_bitcast_fusion.3
  265.8 1.3 exponential_bitcast_fusion.3
  268.2 1.3 exponential_bitcast_fusion.3
  270.6 1.3 exponential_bitcast_fusion.3
  273.0 1.3 exponential_bitcast_fusion.3
  275.3 1.3 exponential_bitcast_fusion.3
  277.7 1.3 exponential_bitcast_fusion.3
  280.1 1.3 exponential_bitcast_fusion.3
  282.4 1.2 exponential_bitcast_fusion.3
  284.8 1.2 exponential_bitcast_fusion.3
  287.1 1.2 exponential_bitcast_fusion.3
  289.4 1.2 exponential_bitcast_fusion.3
  291.8 1.2 exponential_bitcast_fusion.3
  298.7 1.2 exponential_bitcast_fusion.3
  301.1 2.5 fusion.18
  303.6 3.2 multiply_reduce_fusion.1
  310.2 3.8 all-to-all-start
  314.2 5.8 %all-to-all-done = bf16[4,32,1344]{2,1,0:T(8,128)(2,1)S(1)} async-done(((bf16[4,32,1344]{2,1,0:T(8,128)(2,1)}), bf16[4,32,1344]{2,1,0:T(8,128)(2,1)S(1)}, u32[]{:S(2)}, u32[]{:S(2)}) %all-to-all-start) | async-done | bytes 344096 | tf_op jit(solution)/shard_map/all_to_all | solution.py:56
  320.3 1.7 convolution_convert_fusion.1
  322.0 2.5 copy.127
  324.5 46.6 %all_to_all.15 = bf16[32,16,1344]{2,1,0:T(8,128)(2,1)} all-to-all(bf16[32,16,1344]{2,1,0:T(8,128)(2,1)} %bitcast.163), channel_id=1, replica_groups=mesh['seq'=32,'head'=4,'exp'=8] {'head','exp'}, dimensions={0} | all-to-all | bytes 2752512 | tf_op jit(solution)/shard_map/all_to_all | solution.py:211
  371.1 7.2 %convolution_convert_fusion = bf16[512,1344]{0,1:T(8,128)(2,1)} fusion(bf16[1,928,1344]{2,1,0:T(8,128)(2,1)} %param.33, bf16[512,1344]{1,0:T(8,128)(2,1)} %bitcast.169, bf16[1,1344,928]{1,2,0:T(8,128)(2,1)} %param.32), kind=kOutput, calls=%fused_computation.12 | convolution fusion | flops 2556444672 | bytes 7741440 | tf_op jit(solution)/shard_map/dot_general | solution.py:99
  378.3 2.5 copy.128
  380.8 4.5 %all-to-all-start.2 = ((bf16[32,16,1344]{2,1,0:T(8,128)(2,1)}), bf16[32,16,1344]{2,1,0:T(8,128)(2,1)}, u32[]{:S(2)}, u32[]{:S(2)}) async-start(bf16[32,16,1344]{2,1,0:T(8,128)(2,1)} %bitcast.162), calls=%async_computation.2 | async-start | bytes 2883584 | tf_op jit(solution)/shard_map/all_to_all | solution.py:215
  385.7 20.7 %all-to-all-done.2 = bf16[32,16,1344]{2,1,0:T(8,128)(2,1)} async-done(((bf16[32,16,1344]{2,1,0:T(8,128)(2,1)}), bf16[32,16,1344]{2,1,0:T(8,128)(2,1)}, u32[]{:S(2)}, u32[]{:S(2)}) %all-to-all-start.2) | async-done | bytes 1376288 | tf_op jit(solution)/shard_map/all_to_all | solution.py:215
  406.3 3.1 gather_fusion
  409.4 1.2 reshape.248
  410.7 1.9 multiply_reduce_fusion
  412.6 1.6 fusion.48
  (168 shorter events, 80.6 us)
Async XLA Ops:
  6.5 301.9 %copy-start = (bf16[1024,1344]{0,1:T(8,128)(2,1)S(1)}, bf16[1024,1344]{0,1:T(8,128)(2,1)}, u32[]{:S(2)}) copy-start(bf16[1024,1344]{0,1:T(8,128)(2,1)} %param.27) | copy-start | bytes 8257540
  6.5 59.8 %all-gather.5.cloned.1.call-start = ((), (), s32[]{:S(2)}) async-start(), calls=%async_computation.3 | async-start | bytes 2396160 | tf_op jit(solution)/shard_map/all_gather | solution.py:18
  10.6 1.5 copy-start.3
  12.0 0.8 copy-start.2
  14.3 211.5 %all-gather.7.cloned.1.call-start = ((), (), s32[]{:S(2)}) async-start(), calls=%async_computation.4 | async-start | bytes 8650752 | tf_op jit(solution)/shard_map/all_gather | solution.py:28
  68.6 2.7 slice-start
  71.4 20.3 %copy-start.12 = (s32[1,32,6]{1,0,2:T(1,128)S(1)}, s32[1,32,6]{1,0,2:T(1,128)}, u32[]{:S(2)}) copy-start(s32[1,32,6]{1,0,2:T(1,128)} %param.29) | copy-start | bytes 2308
  71.4 24.7 %copy-start.8 = (bf16[128,256]{1,0:T(8,128)(2,1)S(1)}, bf16[128,256]{1,0:T(8,128)(2,1)}, u32[]{:S(2)}) copy-start(bf16[128,256]{1,0:T(8,128)(2,1)} %param.22) | copy-start | bytes 196612
  89.0 136.7 %copy-start.6 = (f32[128,16]{0,1:T(8,128)}, f32[128,16]{0,1:T(8,128)S(1)}, u32[]{:S(2)}) copy-start(f32[128,16]{0,1:T(8,128)S(1)} %copy.116) | copy-start | bytes 24580
  92.8 132.9 %copy-start.9 = (s32[192]{0:T(256)}, s32[192]{0:T(256)S(1)}, u32[]{:S(2)}) copy-start(s32[192]{0:T(256)S(1)} %fusion.54) | copy-start | bytes 2308
  96.2 0.8 copy-start.1
  225.8 77.8 %copy-start.4 = (bf16[128,1024]{0,1:T(8,128)(2,1)S(1)}, bf16[128,1024]{0,1:T(8,128)(2,1)}, u32[]{:S(2)}) copy-start(bf16[128,1024]{0,1:T(8,128)(2,1)} %copy-done.3) | copy-start | bytes 786436
  308.4 5.6 %copy-start.7 = (s32[32,6]{1,0:T(8,128)S(1)}, s32[32,6]{1,0:T(8,128)}, u32[]{:S(2)}) copy-start(s32[32,6]{1,0:T(8,128)} %reduce_sum.88) | copy-start | bytes 2308
  308.4 11.7 %copy-start.5 = (bf16[1,32,1344]{2,1,0:T(8,128)(2,1)S(1)}, bf16[1,32,1344]{2,1,0:T(8,128)(2,1)}, u32[]{:S(2)}) copy-start(bf16[1,32,1344]{2,1,0:T(8,128)(2,1)} %param.28) | copy-start | bytes 258052
  308.4 11.8 %copy-start.11 = (f32[1344]{0:T(1024)S(1)}, f32[1344]{0:T(1024)}, u32[]{:S(2)}) copy-start(f32[1344]{0:T(1024)} %param.31) | copy-start | bytes 16132
  310.2 9.8 %all-to-all-start = ((bf16[4,32,1344]{2,1,0:T(8,128)(2,1)}), bf16[4,32,1344]{2,1,0:T(8,128)(2,1)S(1)}, u32[]{:S(2)}, u32[]{:S(2)}) async-start(bf16[4,32,1344]{2,1,0:T(8,128)(2,1)} %bitcast.19), calls=%async_computation | async-start | bytes 720896 | tf_op jit(solution)/shard_map/all_to_all | solution.py:56
  378.3 7.0 %copy-start.10 = (s32[192]{0:T(256)S(1)}, s32[192]{0:T(256)}, u32[]{:S(2)}) copy-start(s32[192]{0:T(256)} %copy-done.9) | copy-start | bytes 2308
  378.3 7.3 %copy-start.13 = (f32[1,32,6]{1,0,2:T(1,128)S(1)}, f32[1,32,6]{1,0,2:T(1,128)}, u32[]{:S(2)}) copy-start(f32[1,32,6]{1,0,2:T(1,128)} %param.30) | copy-start | bytes 2308
  380.8 25.5 %all-to-all-start.2 = ((bf16[32,16,1344]{2,1,0:T(8,128)(2,1)}), bf16[32,16,1344]{2,1,0:T(8,128)(2,1)}, u32[]{:S(2)}, u32[]{:S(2)}) async-start(bf16[32,16,1344]{2,1,0:T(8,128)(2,1)} %bitcast.162), calls=%async_computation.2 | async-start | bytes 2883584 | tf_op jit(solution)/shard_map/all_to_all | solution.py:215
Sparse Core Ops, SparseCore 0:
  14.4 51.8 all-gather.4
  89.1 136.6 all-gather.6
where the time goes:
time: 424 us; the launch traced here: 421 us
  waiting for transfers between devices  156 us (37%)
  other arithmetic  104 us (25%)
  blocking collectives  95.5 us (23%)
  local copies, waits for them, and re-layouts  25.3 us (6%)
  matrix products  17 us (4%)
  between operations  14.4 us (3%)
  starting transfers between devices  8.31 us (2%)
    all_gather x1, waiting for transfers between devices, prefix(): lax.all_gather(part.astype(kind), axis)  77.1 us
    all_gather x1, waiting for transfers between devices, side_by_side(): filled = lax.all_gather(both, axis, axis=dim, tiled=True)  52 us
    unnamed x1, blocking collectives  48.9 us
    all_to_all x1, blocking collectives, per_device(): lax.all_to_all(outbound, ('head', 'exp'), split_axis=0, concat_axis=0, ti...  46.6 us
    exp x40, other arithmetic, join_pairs(): jnp.exp(later[0])[:, None, None] * earlier[1] + later[1]  40 us
    select_n x32, other arithmetic, turn(): return jax.tree.map(lambda a, b: jnp.where(reached, a, b), new, before)  34.9 us
    all_to_all x1, waiting for transfers between devices, per_device(): lax.all_to_all(produced, ('head', 'exp'), split_axis=0, concat_axis=0, ti...  20.7 us
    add x8, other arithmetic, join_pairs(): jnp.exp(later[0])[:, None, None] * earlier[1] + later[1]  9.26 us
  transfers between devices with their start and end apart: 4, of which 4 were waited for; matrix products, arithmetic and copies ran while one was open for 2% of the time, Pallas kernels for 0%

commit v1 on v0

v1 whole, which is shorter than its diff:
```python
import functools

import jax
import jax.numpy as jnp
from jax import lax
from jax.experimental import pallas as pl
from jax.experimental.pallas import tpu as pltpu
from jax.sharding import PartitionSpec as P

HEAD_DIM = 64
STATE = 128
ROOM = 16
NEAR = 4
F32 = jnp.float32
BF16 = jnp.bfloat16
MESH = pl.DeviceIdType.MESH
EXACT = lax.Precision.HIGHEST


def dot(a, b, ca=1, cb=0, precision=None):
    return lax.dot_general(
        a, b, (((ca,), (cb,)), ((), ())), preferred_element_type=F32, precision=precision
    )


def iota(shape, dim):
    return lax.broadcasted_iota(jnp.int32, shape, dim)


def halves(values):
    high = values.astype(BF16)
    low = (values - high.astype(F32)).astype(BF16)
    return high, low


def kernel(
    sizes,
    x_ref,
    z_ref,
    b_ref,
    c_ref,
    dt_ref,
    alog_ref,
    dskip_ref,
    normw_ref,
    resid_ref,
    routes_ref,
    gates_ref,
    gain_ref,
    wout_hbm,
    wup_hbm,
    wdown_hbm,
    out_ref,
    wout,
    wup,
    wdown,
    wsem,
    y_ref,
    grow_ref,
    pre_ref,
    lpre_ref,
    send_a,
    recv_a,
    sa_sem,
    ra_sem,
    send_n,
    recv_n,
    sn_sem,
    rn_sem,
    pn_ref,
    lpn_ref,
    send_f,
    recv_f,
    sf_sem,
    rf_sem,
    send_m,
    recv_m,
    sm_sem,
    rm_sem,
    send_b,
    recv_b,
    sb_sem,
    rb_sem,
    send_r,
    recv_r,
    sr_sem,
    rr_sem,
    send_d,
    recv_d,
    sd_sem,
    rd_sem,
    send_o,
    recv_o,
    so_sem,
    ro_sem,
):
    n_seq, n_head, n_exp = sizes
    n_far = n_seq // NEAR
    n_plane = n_head * n_exp
    tokens = x_ref.shape[0]
    heads = dt_ref.shape[0]
    groups = b_ref.shape[1] // STATE
    per_group = heads // groups
    width = per_group * HEAD_DIM
    own_heads = heads // n_exp
    own_rows = own_heads * HEAD_DIM
    near_rows = own_rows // NEAR
    rows_here = resid_ref.shape[1]

    me_z = lax.axis_index("seq")
    me_x = lax.axis_index("head")
    me_e = lax.axis_index("exp")
    me_far = me_z // NEAR
    me_near = me_z % NEAR
    me_plane = me_x * n_exp + me_e

    w_copies = [
        pltpu.make_async_copy(wout_hbm, wout, wsem.at[0]),
        pltpu.make_async_copy(wup_hbm, wup, wsem.at[1]),
        pltpu.make_async_copy(wdown_hbm, wdown, wsem.at[2]),
    ]
    for copy in w_copies:
        copy.start()

    def plane_id(d):
        there = lax.rem(me_plane + d, n_plane)
        return there, {"head": there // n_exp, "exp": there % n_exp}

    def exp_id(d):
        there = lax.rem(me_e + d, n_exp)
        return there, {"exp": there}

    def head_id(d):
        there = lax.rem(me_x + d, n_head)
        return there, {"head": there}

    def near_id(d):
        there = lax.rem(me_near + d, NEAR)
        return there, {"seq": me_far * NEAR + there}

    def far_id(d):
        there = lax.rem(me_far + d, n_far)
        return there, {"seq": there * NEAR + me_near}

    barrier = pltpu.get_barrier_semaphore()

    def greet(peer, count):
        def one(d, carry):
            pl.semaphore_signal(barrier, inc=1, device_id=peer(d)[1], device_id_type=MESH)
            return carry

        lax.fori_loop(1, count, one, 0)

    greet(far_id, n_far)
    greet(near_id, NEAR)
    greet(plane_id, n_plane)

    def exchange(peer, count, source, landing, mine, send_sems, recv_sems):
        def copy(there, where):
            return pltpu.make_async_remote_copy(
                src_ref=source.at[there],
                dst_ref=landing.at[mine],
                send_sem=send_sems.at[there],
                recv_sem=recv_sems.at[mine],
                device_id=where,
                device_id_type=MESH,
            )

        def start(d, carry):
            copy(*peer(d)).start()
            return carry

        def sent(d, carry):
            copy(*peer(d)).wait_send()
            return carry

        def arrived(d, carry):
            there, where = peer(d)
            pltpu.make_async_remote_copy(
                src_ref=source.at[there],
                dst_ref=landing.at[there],
                send_sem=send_sems.at[there],
                recv_sem=recv_sems.at[there],
                device_id=where,
                device_id_type=MESH,
            ).wait_recv()
            return carry

        return (
            lambda: lax.fori_loop(1, count, start, 0),
            lambda: lax.fori_loop(1, count, arrived, 0),
            lambda: lax.fori_loop(1, count, sent, 0),
        )

    start_a, arrived_a, sent_a = exchange(exp_id, n_exp, send_a, recv_a, me_e, sa_sem, ra_sem)
    start_n, arrived_n, sent_n = exchange(near_id, NEAR, send_n, recv_n, me_near, sn_sem, rn_sem)
    start_m, arrived_m, sent_m = exchange(near_id, NEAR, send_m, recv_m, me_near, sm_sem, rm_sem)
    start_b, arrived_b, sent_b = exchange(exp_id, n_exp, send_b, recv_b, me_e, sb_sem, rb_sem)
    start_r, arrived_r, sent_r = exchange(head_id, n_head, send_r, recv_r, me_x, sr_sem, rr_sem)
    start_d, arrived_d, sent_d = exchange(
        plane_id, n_plane, send_d, recv_d, me_plane, sd_sem, rd_sem
    )
    start_o, arrived_o, sent_o = exchange(
        plane_id, n_plane, send_o, recv_o, me_plane, so_sem, ro_sem
    )

    dt = dt_ref[...]
    step_t = jnp.maximum(dt, 0.0) + jnp.log1p(jnp.exp(-jnp.abs(dt)))
    decay_rate = jnp.broadcast_to(jnp.exp(alog_ref[...]), (heads, heads))
    same_head = iota((heads, heads), 0) == iota((heads, heads), 1)
    decay_rate = jnp.sum(jnp.where(same_head, decay_rate, 0.0), axis=1, keepdims=True)
    rate_t = -step_t * decay_rate
    row_t, col_t = iota((tokens, tokens), 0), iota((tokens, tokens), 1)
    causal = row_t >= col_t
    upto = jnp.where(causal, 1.0, 0.0)
    cum_t = dot(rate_t, upto, 1, 1, EXACT)
    cum = dot(upto, rate_t, 1, 1, EXACT)
    step = dot(jnp.where(row_t == col_t, 1.0, 0.0), step_t, 1, 1, EXACT)
    tail = jnp.exp(cum[tokens - 1 : tokens, :] - cum) * step
    grow = jnp.exp(cum)
    channels = heads * HEAD_DIM
    spread = jnp.where(
        iota((heads, channels), 1) // HEAD_DIM == iota((heads, channels), 0), 1.0, 0.0
    )
    tail_wide = dot(tail, spread, 1, 0, EXACT)
    weighted = (tail_wide * x_ref[...].astype(F32)).astype(BF16)

    total = jnp.broadcast_to(cum_t[:, tokens - 1 : tokens], (heads, STATE))
    total_high, total_low = halves(total)
    per_send = n_exp // groups
    for g in range(groups):
        update = dot(
            weighted[:, g * width : (g + 1) * width],
            b_ref[:, g * STATE : (g + 1) * STATE],
            0,
            0,
        ).astype(BF16)
        for k in range(per_send):
            send_a[g * per_send + k, 0:own_rows, :] = update[k * own_rows : (k + 1) * own_rows, :]
    for k in range(n_exp):
        send_a[k, own_rows : own_rows + heads, :] = total_high
        send_a[k, own_rows + heads : own_rows + 2 * heads, :] = total_low

    pl.semaphore_wait(barrier, (n_far - 1) + (NEAR - 1) + (n_plane - 1))
    start_a()
    recv_a[me_e] = send_a[me_e]

    first_half = iota((tokens, 2 * HEAD_DIM), 1) < HEAD_DIM
    skip_wide = dot(dskip_ref[...], spread, 1, 0, EXACT)
    for g in range(groups):
        scores = dot(
            c_ref[:, g * STATE : (g + 1) * STATE], b_ref[:, g * STATE : (g + 1) * STATE], 1, 1
        )
        for j in range(g * per_group // 2, (g + 1) * per_group // 2):
            lanes = slice(2 * HEAD_DIM * j, 2 * HEAD_DIM * (j + 1))
            mixes = []
            for h in (2 * j, 2 * j + 1):
                distance = cum[:, h : h + 1] - cum_t[h : h + 1, :]
                decay = jnp.where(causal, jnp.exp(jnp.where(causal, distance, 0.0)), 0.0)
                mixes.append((scores * (decay * step_t[h : h + 1, :])).astype(BF16))
            pair = x_ref[:, lanes]
            zero = jnp.zeros_like(pair)
            stacked = jnp.concatenate(
                [jnp.where(first_half, pair, zero), jnp.where(first_half, zero, pair)], axis=0
            )
            inside = dot(jnp.concatenate(mixes, axis=1), stacked)
            y_ref[:, lanes] = inside + skip_wide[:, lanes] * pair.astype(F32)
    grow_ref[...] = dot(grow, spread, 1, 0, EXACT)

    expert_row = iota((n_plane, rows_here), 0)
    routed = jnp.zeros((n_plane, rows_here), F32)
    gate = jnp.zeros((n_plane, rows_here), F32)
    for k in range(routes_ref.shape[0]):
        hit = expert_row == routes_ref[k : k + 1, :]
        routed = jnp.where(hit, 1.0, routed)
        gate = jnp.where(hit, gates_ref[k : k + 1, :], gate)
    ahead = jnp.where(
        iota((rows_here, rows_here), 0) < iota((rows_here, rows_here), 1), 1.0, 0.0
    ).astype(BF16)
    place = jnp.where(routed > 0.5, dot(routed.astype(BF16), ahead), -1.0)
    slots = n_plane * ROOM
    repeat = jnp.where(
        iota((slots, n_plane), 0) // ROOM == iota((slots, n_plane), 1), 1.0, 0.0
    ).astype(BF16)
    place_wide = dot(repeat, place.astype(BF16))
    chosen = place_wide == (iota((slots, rows_here), 0) % ROOM).astype(F32)
    gate_high, gate_low = halves(gate)
    pick = jnp.where(chosen, 1.0, 0.0).astype(BF16)
    pick_high = jnp.where(chosen, dot(repeat, gate_high), 0.0).astype(BF16)
    pick_low = jnp.where(chosen, dot(repeat, gate_low), 0.0).astype(BF16)

    arrived_a()
    head_row = iota((heads, STATE), 0)
    own_row = iota((own_rows, STATE), 0)
    state = jnp.zeros((own_rows, STATE), F32)
    log_sum = jnp.zeros((own_rows, STATE), F32)
    for k in range(n_exp):
        pre_ref[k] = state
        lpre_ref[k] = log_sum
        high = recv_a[k, own_rows : own_rows + heads, :].astype(F32)
        low = recv_a[k, own_rows + heads : own_rows + 2 * heads, :].astype(F32)
        both = high + low
        log_here = jnp.zeros((own_rows, STATE), F32)
        for h in range(own_heads):
            one = jnp.sum(
                jnp.where(head_row == me_e * own_heads + h, both, 0.0), axis=0, keepdims=True
            )
            log_here = jnp.where(own_row // HEAD_DIM == h, one, log_here)
        state = jnp.exp(log_here) * state + recv_a[k, 0:own_rows, :].astype(F32)
        log_sum = log_sum + log_here

    def packed(values, logs):
        high, low = halves(logs)
        tile = jnp.where(
            iota((16, STATE), 0) < 8,
            jnp.broadcast_to(high.astype(F32), (16, STATE)),
            jnp.broadcast_to(low.astype(F32), (16, STATE)),
        )
        return values.astype(BF16), tile.astype(BF16)

    def unpacked(ref, k):
        tile = ref[k, near_rows : near_rows + 16, :].astype(F32)
        return ref[k, 0:near_rows, :].astype(F32), tile[0:1, :] + tile[8:9, :]

    for k in range(NEAR):
        rows = slice(k * near_rows, (k + 1) * near_rows)
        values, tile = packed(state[rows], log_sum[k * near_rows : k * near_rows + 1])
        send_n[k, 0:near_rows, :] = values
        send_n[k, near_rows : near_rows + 16, :] = tile
    start_n()
    recv_n[me_near] = send_n[me_near]
    arrived_n()
    part = jnp.zeros((near_rows, STATE), F32)
    part_log = jnp.zeros((1, STATE), F32)
    for k in range(NEAR):
        pn_ref[k] = part
        lpn_ref[k] = jnp.broadcast_to(part_log, (8, STATE))
        values, log_here = unpacked(recv_n, k)
        part = jnp.exp(log_here) * part + values
        part_log = part_log + log_here
    values, tile = packed(part, part_log)
    send_f[0:near_rows, :] = values
    send_f[near_rows : near_rows + 16, :] = tile

    def far_copy(there, slot):
        return pltpu.make_async_remote_copy(
            src_ref=send_f,
            dst_ref=recv_f.at[slot],
            send_sem=sf_sem.at[there],
            recv_sem=rf_sem.at[slot],
            device_id={"seq": there * NEAR + me_near},
            device_id_type=MESH,
        )

    def far_start(k, carry):
        far_copy(k, me_far).start()
        return carry

    lax.fori_loop(me_far + 1, n_far, far_start, 0)

    def far_fold(k, carry):
        far_copy(k, k).wait_recv()
        values, log_here = unpacked(recv_f, k)
        return jnp.exp(log_here) * carry + values

    chain = lax.fori_loop(0, me_far, far_fold, jnp.zeros((near_rows, STATE), F32))

    for k in range(NEAR):
        send_m[k] = (jnp.exp(lpn_ref[k, 0:1, :]) * chain + pn_ref[k]).astype(BF16)
    start_m()
    recv_m[me_near] = send_m[me_near]
    arrived_m()
    chain_in = recv_m[...].astype(F32).reshape(own_rows, STATE)
    for k in range(n_exp):
        send_b[k] = (jnp.exp(lpre_ref[k]) * chain_in + pre_ref[k]).astype(BF16)
    start_b()
    recv_b[me_e] = send_b[me_e]
    arrived_b()

    before = recv_b[...].reshape(channels, STATE)
    normed = []
    for g in range(groups):
        lanes = slice(g * width, (g + 1) * width)
        carried = dot(c_ref[:, g * STATE : (g + 1) * STATE], before[lanes], 1, 1)
        ssm_out = y_ref[:, lanes] + grow_ref[:, lanes] * carried
        z_here = z_ref[:, lanes].astype(F32)
        gated = ssm_out * (z_here / (1.0 + jnp.exp(-z_here)))
        inverse = lax.rsqrt(jnp.mean(gated * gated, axis=1, keepdims=True) + 1e-05)
        normed.append((gated * inverse * normw_ref[:, lanes]).astype(BF16))
    normed = jnp.concatenate(normed, axis=1)
    w_copies[0].wait()
    projected = dot(normed, wout[...], 1, 1).astype(BF16)
    for k in range(n_head):
        send_r[k] = projected[k * rows_here : (k + 1) * rows_here]
    start_r()
    recv_r[me_x] = send_r[me_x]
    arrived_r()
    mixed = jnp.sum(recv_r[...].astype(F32), axis=0)
    hidden = (resid_ref[0].astype(F32) + mixed).astype(BF16).astype(F32)
    scale = lax.rsqrt(jnp.mean(hidden * hidden, axis=1, keepdims=True) + 1e-05)
    moe_in = (hidden * scale * gain_ref[...]).astype(BF16)

    model = moe_in.shape[1]
    send_d[...] = dot(pick, moe_in).astype(BF16).reshape(n_plane, ROOM, model)
    start_d()
    recv_d[me_plane] = send_d[me_plane]
    arrived_d()
    w_copies[1].wait()
    w_copies[2].wait()
    rows = recv_d[...].reshape(slots, model)
    raised = jnp.maximum(dot(rows, wup[0], 1, 1), 0.0)
    activated = (raised * raised).astype(BF16)
    send_o[...] = dot(activated, wdown[0]).astype(BF16).reshape(n_plane, ROOM, model)
    start_o()
    recv_o[me_plane] = send_o[me_plane]
    arrived_o()
    returned = recv_o[...].reshape(slots, model)
    moe_sum = dot(pick_high, returned, 0, 0) + dot(pick_low, returned, 0, 0)
    out_ref[0] = (hidden + moe_sum).astype(BF16)

    for sent in (sent_a, sent_n, sent_m, sent_b, sent_r, sent_d, sent_o):
        sent()

    def far_sent(k, carry):
        far_copy(k, me_far).wait_send()
        return carry

    lax.fori_loop(me_far + 1, n_far, far_sent, 0)


def per_device(
    sizes,
    x_in,
    z_in,
    b_in,
    c_in,
    dt_in,
    a_log,
    d_skip,
    norm_w,
    w_out,
    resid,
    routes,
    gates,
    moe_gain,
    w_up,
    w_down,
):
    n_seq, n_head, n_exp = sizes
    n_far, n_plane = n_seq // NEAR, n_head * n_exp
    tokens, heads = dt_in.shape
    channels = heads * HEAD_DIM
    own_rows = channels // n_exp
    near_rows = own_rows // NEAR
    rows_here, model = resid.shape[1:]
    dma = pltpu.SemaphoreType.DMA
    vmem = pl.BlockSpec(memory_space=pltpu.VMEM)
    hbm = pl.BlockSpec(memory_space=pl.ANY)
    w_out_t = w_out.T
    w_up_t = w_up.transpose(0, 2, 1)
    scratch = [
        pltpu.VMEM(w_out_t.shape, BF16),
        pltpu.VMEM(w_up_t.shape, BF16),
        pltpu.VMEM(w_down.shape, BF16),
        dma((3,)),
        pltpu.VMEM((tokens, channels), F32),
        pltpu.VMEM((tokens, channels), F32),
        pltpu.VMEM((n_exp, own_rows, STATE), F32),
        pltpu.VMEM((n_exp, own_rows, STATE), F32),
    ]

    def pair(count, *block):
        return [
            pltpu.VMEM((count, *block), BF16),
            pltpu.VMEM((count, *block), BF16),
            dma((count,)),
            dma((count,)),
        ]

    scratch += pair(n_exp, own_rows + 2 * heads, STATE)
    scratch += pair(NEAR, near_rows + 16, STATE)
    scratch += [
        pltpu.VMEM((NEAR, near_rows, STATE), F32),
        pltpu.VMEM((NEAR, 8, STATE), F32),
        pltpu.VMEM((near_rows + 16, STATE), BF16),
        pltpu.VMEM((n_far, near_rows + 16, STATE), BF16),
        dma((n_far,)),
        dma((n_far,)),
    ]
    scratch += pair(NEAR, near_rows, STATE)
    scratch += pair(n_exp, own_rows, STATE)
    scratch += pair(n_head, rows_here, model)
    scratch += pair(n_plane, ROOM, model)
    scratch += pair(n_plane, ROOM, model)
    return pl.pallas_call(
        functools.partial(kernel, sizes),
        out_shape=jax.ShapeDtypeStruct(resid.shape, BF16),
        in_specs=[vmem] * 12 + [hbm] * 3,
        out_specs=vmem,
        scratch_shapes=scratch,
        compiler_params=pltpu.CompilerParams(
            collective_id=0, has_side_effects=True, vmem_limit_bytes=60 * 2**20
        ),
    )(
        x_in,
        z_in,
        b_in,
        c_in,
        dt_in.T,
        a_log.reshape(1, heads),
        d_skip.reshape(1, heads),
        norm_w.reshape(1, channels),
        resid,
        routes[0].T,
        gates[0].T,
        moe_gain.reshape(1, model),
        w_out_t,
        w_up_t,
        w_down,
    )


def solution(mesh):
    sizes = (mesh.shape["seq"], mesh.shape["head"], mesh.shape["exp"])
    placed = (
        P(("seq", "exp"), "head"),
        P(("seq", "exp"), "head"),
        P(("seq", "exp"), "head"),
        P(("seq", "exp"), "head"),
        P(("seq", "exp"), "head"),
        P("head"),
        P("head"),
        P("head"),
        P("head", None),
        P(("seq", "exp"), "head", None),
        P(("seq", "exp"), "head", None),
        P(("seq", "exp"), "head", None),
        P(),
        P(("head", "exp"), None, None),
        P(("head", "exp"), None, None),
    )
    return jax.shard_map(
        functools.partial(per_device, sizes),
        mesh=mesh,
        in_specs=placed,
        out_specs=P(("seq", "exp"), "head", None),
        check_vma=False,
    )
```

time: 424 us -> 119 us (0.28)
  waiting for transfers between devices: 156 us -> 0 us
  Pallas kernels: 0 us -> 112 us
  other arithmetic: 104 us -> 0 us
  blocking collectives: 95.5 us -> 0 us
  local copies, waits for them, and re-layouts: 25.3 us -> 5.38 us
  matrix products: 17 us -> 0 us
  between operations: 14.4 us -> 0.01 us
  starting transfers between devices: 8.31 us -> 0 us
    all_gather x2 -> x0, waiting for transfers between devices: 129 us -> none  [the longest x1 77.1 us: prefix(): lax.all_gather(part.astype(kind), axis)]
    pallas_call x0 -> x1, Pallas kernels: none -> 112 us  [per_device(): pl.pallas_call(functools.partial(kernel, sizes), out_shape=jax.ShapeDtype...]
    unnamed x1 -> x0, blocking collectives: 48.9 us -> none
    all_to_all x1 -> x0, blocking collectives: 46.6 us -> none  [per_device(): lax.all_to_all(outbound, ('head', 'exp'), split_axis=0, concat_axis=0, ti...]
    exp x40 -> x0, other arithmetic: 40 us -> none  [join_pairs(): jnp.exp(later[0])[:, None, None] * earlier[1] + later[1]]
    select_n x33 -> x0, other arithmetic: 34.9 us -> none  [the longest x32 34.9 us: turn(): return jax.tree.map(lambda a, b: jnp.where(reached, a, b), new, before)]
    all_to_all x2 -> x0, waiting for transfers between devices: 26.5 us -> none  [the longest x1 20.7 us: per_device(): lax.all_to_all(produced, ('head', 'exp'), split_axis=0, concat_axis=0, ti...]
    dot_general x7 -> x0, matrix products: 17 us -> none  [the longest x1 7.16 us: expert_rows(): jnp.dot(activated, w_down[0], preferred_element_type=jnp.float32)]
  transfers between devices with their start and end apart: 4 -> 0, of which waited for: 4 -> 0; matrix products, arithmetic and copies ran while one was open for 2% -> 0% of each run, Pallas kernels for 0% -> 0%
where the time goes in v1:
time: 119 us; the launch traced here: 117 us
  Pallas kernels  112 us (94%)
  local copies, waits for them, and re-layouts  5.38 us (5%)
    pallas_call x1, Pallas kernels, per_device(): pl.pallas_call(functools.partial(kernel, sizes), out_shape=jax.ShapeDtype...  112 us
    unnamed x3, local copies, waits for them, and re-layouts  4.09 us

profile of v1, /device:TPU:1, one launch (start us, length us, event | category | flops | bytes accessed | tf_op | source)
XLA Modules:
  0.0 116.9 jit_solution(14241020748729222107)
XLA Ops:
  0.0 1.3 %copy.21 = s32[1,32,6]{1,2,0:T(8,128)} copy(s32[1,32,6]{1,0,2:T(1,128)} %param.25) | data formatting | bytes 1536
  1.3 1.3 %copy.20 = f32[1,32,6]{1,2,0:T(8,128)} copy(f32[1,32,6]{1,0,2:T(1,128)} %param.26) | data formatting | bytes 1536
  2.6 1.3 %reshape.15.gain_ref = f32[1,1344]{1,0:T(1,128)} reshape(f32[1344]{0:T(1024)} %param.27) | data formatting | bytes 10752 | tf_op jit(solution)/shard_map/reshape | solution.py:516
  3.9 111.6 %shard_map.145 = bf16[1,32,1344]{2,1,0:T(8,128)(2,1)} custom-call(bf16[128,1024]{1,0:T(8,128)(2,1)} %x_ref.1, bf16[128,1024]{1,0:T(8,128)(2,1)} %z_ref.1, bf16[128,256]{1,0:T(8,128)(2,1)} %b_ref.1, bf16[128,256]{1,0:T(8,128)(2,1)} %c_ref.1, f32[16,128]{1,0:T(8,128)} %bitcast.20, f32[1,16]{1,0:T(1,128)} %bitcast.22, f32[1,16]{1,0:T(1,128)} %bitcast.23, ...), custom_call_target="tpu_custom_call" | custom-call | tf_op jit(solution)/shard_map/pallas_call | solution.py:495
  115.4 1.5 %copy.23 = bf16[1,32,1344]{2,1,0:T(8,128)(2,1)} copy(bf16[1,32,1344]{2,1,0:T(8,128)(2,1)} %shard_map.145) | data formatting | bytes 172032

commit v2 on v1

--- a/solution.py
+++ b/solution.py
@@ -13,6 +13,7 @@
 NEAR = 4
 F32 = jnp.float32
 BF16 = jnp.bfloat16
+REACH = (1, 2, -1, -2)
 MESH = pl.DeviceIdType.MESH
 EXACT = lax.Precision.HIGHEST
 
@@ -96,6 +97,7 @@
 ):
     n_seq, n_head, n_exp = sizes
     n_far = n_seq // NEAR
+    assert n_far in (1, 8)
     n_plane = n_head * n_exp
     tokens = x_ref.shape[0]
     heads = dt_ref.shape[0]
@@ -139,8 +141,8 @@
         return there, {"seq": me_far * NEAR + there}
 
     def far_id(d):
-        there = lax.rem(me_far + d, n_far)
-        return there, {"seq": there * NEAR + me_near}
+        there = lax.rem(me_far + d + n_far, n_far)
+        return {"seq": there * NEAR + me_near}
 
     barrier = pltpu.get_barrier_semaphore()
 
@@ -151,7 +153,9 @@
 
         lax.fori_loop(1, count, one, 0)
 
-    greet(far_id, n_far)
+    if n_far > 1:
+        for d in REACH:
+            pl.semaphore_signal(barrier, inc=1, device_id=far_id(d), device_id_type=MESH)
     greet(near_id, NEAR)
     greet(plane_id, n_plane)
 
@@ -241,7 +245,7 @@
         send_a[k, own_rows : own_rows + heads, :] = total_high
         send_a[k, own_rows + heads : own_rows + 2 * heads, :] = total_low
 
-    pl.semaphore_wait(barrier, (n_far - 1) + (NEAR - 1) + (n_plane - 1))
+    pl.semaphore_wait(barrier, (len(REACH) if n_far > 1 else 0) + (NEAR - 1) + (n_plane - 1))
     start_a()
     recv_a[me_e] = send_a[me_e]
 
@@ -271,9 +275,9 @@
     routed = jnp.zeros((n_plane, rows_here), F32)
     gate = jnp.zeros((n_plane, rows_here), F32)
     for k in range(routes_ref.shape[0]):
-        hit = expert_row == routes_ref[k : k + 1, :]
+        hit = expert_row == routes_ref[k]
         routed = jnp.where(hit, 1.0, routed)
-        gate = jnp.where(hit, gates_ref[k : k + 1, :], gate)
+        gate = jnp.where(hit, gates_ref[k], gate)
     ahead = jnp.where(
         iota((rows_here, rows_here), 0) < iota((rows_here, rows_here), 1), 1.0, 0.0
     ).astype(BF16)
@@ -338,32 +342,48 @@
         values, log_here = unpacked(recv_n, k)
         part = jnp.exp(log_here) * part + values
         part_log = part_log + log_here
-    values, tile = packed(part, part_log)
-    send_f[0:near_rows, :] = values
-    send_f[near_rows : near_rows + 16, :] = tile
-
-    def far_copy(there, slot):
+    chain = jnp.zeros((near_rows, STATE), F32)
+
+    def put(slot, values, logs):
+        values, tile = packed(values, logs)
+        send_f[slot, 0:near_rows, :] = values
+        send_f[slot, near_rows : near_rows + 16, :] = tile
+
+    def far_copy(d, source, slot):
         return pltpu.make_async_remote_copy(
-            src_ref=send_f,
+            src_ref=send_f.at[source],
             dst_ref=recv_f.at[slot],
-            send_sem=sf_sem.at[there],
+            send_sem=sf_sem.at[slot],
             recv_sem=rf_sem.at[slot],
-            device_id={"seq": there * NEAR + me_near},
+            device_id=far_id(d),
             device_id_type=MESH,
         )
 
-    def far_start(k, carry):
-        far_copy(k, me_far).start()
-        return carry
-
-    lax.fori_loop(me_far + 1, n_far, far_start, 0)
-
-    def far_fold(k, carry):
-        far_copy(k, k).wait_recv()
-        values, log_here = unpacked(recv_f, k)
-        return jnp.exp(log_here) * carry + values
-
-    chain = lax.fori_loop(0, me_far, far_fold, jnp.zeros((near_rows, STATE), F32))
+    if n_far > 1:
+        put(0, part, part_log)
+        copies = [far_copy(d, 0, slot) for slot, d in enumerate(REACH)]
+        for copy in copies:
+            copy.start()
+        for copy in copies[:3]:
+            copy.wait_recv()
+        one, one_log = unpacked(recv_f, 0)
+        two, two_log = unpacked(recv_f, 1)
+        two = jnp.where(me_far >= 2, two, 0.0)
+        two_log = jnp.where(me_far >= 2, two_log, 0.0)
+        fold = jnp.where(me_far >= 1, jnp.exp(one_log) * two + one, 0.0)
+        fold_log = jnp.where(me_far >= 1, one_log + two_log, 0.0)
+        put(1, fold, fold_log)
+        copies.append(far_copy(2, 1, 4))
+        copies[4].start()
+        back, back_log = unpacked(recv_f, 2)
+        put(2, back, back_log)
+        copies.append(far_copy(-2, 2, 5))
+        copies[5].start()
+        for copy in copies[3:]:
+            copy.wait_recv()
+        for slot, least in ((2, 7), (3, 6), (5, 5), (4, 2), (1, 2), (0, 1)):
+            values, log_here = unpacked(recv_f, slot)
+            chain = jnp.where(me_far >= least, jnp.exp(log_here) * chain + values, chain)
 
     for k in range(NEAR):
         send_m[k] = (jnp.exp(lpn_ref[k, 0:1, :]) * chain + pn_ref[k]).astype(BF16)
@@ -398,7 +418,7 @@
     mixed = jnp.sum(recv_r[...].astype(F32), axis=0)
     hidden = (resid_ref[0].astype(F32) + mixed).astype(BF16).astype(F32)
     scale = lax.rsqrt(jnp.mean(hidden * hidden, axis=1, keepdims=True) + 1e-05)
-    moe_in = (hidden * scale * gain_ref[...]).astype(BF16)
+    moe_in = (hidden * scale * gain_ref[...].reshape(1, -1)).astype(BF16)
 
     model = moe_in.shape[1]
     send_d[...] = dot(pick, moe_in).astype(BF16).reshape(n_plane, ROOM, model)
@@ -421,11 +441,9 @@
     for sent in (sent_a, sent_n, sent_m, sent_b, sent_r, sent_d, sent_o):
         sent()
 
-    def far_sent(k, carry):
-        far_copy(k, me_far).wait_send()
-        return carry
-
-    lax.fori_loop(me_far + 1, n_far, far_sent, 0)
+    if n_far > 1:
+        for copy in copies:
+            copy.wait_send()
 
 
 def per_device(
@@ -447,7 +465,7 @@
     w_down,
 ):
     n_seq, n_head, n_exp = sizes
-    n_far, n_plane = n_seq // NEAR, n_head * n_exp
+    n_plane = n_head * n_exp
     tokens, heads = dt_in.shape
     channels = heads * HEAD_DIM
     own_rows = channels // n_exp
@@ -482,10 +500,10 @@
     scratch += [
         pltpu.VMEM((NEAR, near_rows, STATE), F32),
         pltpu.VMEM((NEAR, 8, STATE), F32),
-        pltpu.VMEM((near_rows + 16, STATE), BF16),
-        pltpu.VMEM((n_far, near_rows + 16, STATE), BF16),
-        dma((n_far,)),
-        dma((n_far,)),
+        pltpu.VMEM((3, near_rows + 16, STATE), BF16),
+        pltpu.VMEM((6, near_rows + 16, STATE), BF16),
+        dma((6,)),
+        dma((6,)),
     ]
     scratch += pair(NEAR, near_rows, STATE)
     scratch += pair(n_exp, own_rows, STATE)
@@ -511,9 +529,9 @@
         d_skip.reshape(1, heads),
         norm_w.reshape(1, channels),
         resid,
-        routes[0].T,
-        gates[0].T,
-        moe_gain.reshape(1, model),
+        routes.transpose(2, 0, 1),
+        gates.transpose(2, 0, 1),
+        moe_gain,
         w_out_t,
         w_up_t,
         w_down,

time: 119 us -> 119 us (level)
  the two profiles are of different devices: /device:TPU:1 before, /device:TPU:25 now
where the time goes in v2:
time: 119 us
  Pallas kernels  118 us (99%)
  local copies, waits for them, and re-layouts  1.54 us (1%)
    pallas_call x1, Pallas kernels, per_device(): pl.pallas_call(functools.partial(kernel, sizes), out_shape=jax.ShapeDtype...  118 us

profile of v2, /device:TPU:25, one launch (start us, length us, event | category | flops | bytes accessed | tf_op | source)
XLA Modules:
  0.0 119.1 jit_solution(855948308478523228)
XLA Ops:
  0.0 117.6 %shard_map.145 = bf16[1,32,1344]{2,1,0:T(8,128)(2,1)} custom-call(bf16[128,1024]{1,0:T(8,128)(2,1)} %x_ref.1, bf16[128,1024]{1,0:T(8,128)(2,1)} %z_ref.1, bf16[128,256]{1,0:T(8,128)(2,1)} %b_ref.1, bf16[128,256]{1,0:T(8,128)(2,1)} %c_ref.1, f32[16,128]{1,0:T(8,128)} %bitcast.10, f32[1,16]{1,0:T(1,128)} %bitcast.14, f32[1,16]{1,0:T(1,128)} %bitcast.15, ...), custom_call_target="tpu_custom_call" | custom-call | tf_op jit(solution)/shard_map/pallas_call | solution.py:513
  117.6 1.5 %copy.17 = bf16[1,32,1344]{2,1,0:T(8,128)(2,1)} copy(bf16[1,32,1344]{2,1,0:T(8,128)(2,1)} %shard_map.145) | data formatting | bytes 172032

commit v3 on v2

--- a/solution.py
+++ b/solution.py
@@ -10,6 +10,7 @@
 HEAD_DIM = 64
 STATE = 128
 ROOM = 16
+CORES = 2
 NEAR = 4
 F32 = jnp.float32
 BF16 = jnp.bfloat16
@@ -86,14 +87,48 @@
     recv_r,
     sr_sem,
     rr_sem,
-    send_d,
-    recv_d,
-    sd_sem,
-    rd_sem,
-    send_o,
-    recv_o,
-    so_sem,
-    ro_sem,
+    table_x,
+    tables_x,
+    tx_send,
+    tx_recv,
+    table_y,
+    tables_y,
+    ty_send,
+    ty_recv,
+    pick_x,
+    pick_y,
+    half_x,
+    gathered_x,
+    gx_send,
+    gx_recv,
+    half_y,
+    gathered_y,
+    gy_send,
+    gy_recv,
+    rows_x,
+    landed_x,
+    lx_send,
+    lx_recv,
+    rows_y,
+    landed_y,
+    ly_send,
+    ly_recv,
+    made_x,
+    back_x,
+    bx_send,
+    bx_recv,
+    made_y,
+    back_y,
+    by_send,
+    by_recv,
+    sums_x,
+    last_x,
+    fx_send,
+    fx_recv,
+    sums_y,
+    last_y,
+    fy_send,
+    fy_recv,
 ):
     n_seq, n_head, n_exp = sizes
     n_far = n_seq // NEAR
@@ -114,7 +149,10 @@
     me_e = lax.axis_index("exp")
     me_far = me_z // NEAR
     me_near = me_z % NEAR
-    me_plane = me_x * n_exp + me_e
+    n_y = n_exp // CORES
+    me_y = me_e // CORES
+    me_c = me_e % CORES
+    me_block = me_x * CORES + me_c
 
     w_copies = [
         pltpu.make_async_copy(wout_hbm, wout, wsem.at[0]),
@@ -124,10 +162,6 @@
     for copy in w_copies:
         copy.start()
 
-    def plane_id(d):
-        there = lax.rem(me_plane + d, n_plane)
-        return there, {"head": there // n_exp, "exp": there % n_exp}
-
     def exp_id(d):
         there = lax.rem(me_e + d, n_exp)
         return there, {"exp": there}
@@ -135,6 +169,14 @@
     def head_id(d):
         there = lax.rem(me_x + d, n_head)
         return there, {"head": there}
+
+    def y_id(d):
+        there = lax.rem(me_y + d, n_y)
+        return there, {"exp": there * CORES + me_c}
+
+    def block_id(d):
+        there = lax.rem(me_block + d, n_head * CORES)
+        return there, {"head": there // CORES, "exp": me_y * CORES + there % CORES}
 
     def near_id(d):
         there = lax.rem(me_near + d, NEAR)
@@ -157,37 +199,36 @@
         for d in REACH:
             pl.semaphore_signal(barrier, inc=1, device_id=far_id(d), device_id_type=MESH)
     greet(near_id, NEAR)
-    greet(plane_id, n_plane)
+    greet(exp_id, n_exp)
+    for d in range(1, n_head):
+        for core in range(CORES):
+            where = {"head": lax.rem(me_x + d, n_head), "exp": me_y * CORES + core}
+            pl.semaphore_signal(barrier, inc=1, device_id=where, device_id_type=MESH)
 
     def exchange(peer, count, source, landing, mine, send_sems, recv_sems):
-        def copy(there, where):
+        def copy(there, where, place):
             return pltpu.make_async_remote_copy(
-                src_ref=source.at[there],
-                dst_ref=landing.at[mine],
+                src_ref=source(there),
+                dst_ref=landing(place),
                 send_sem=send_sems.at[there],
-                recv_sem=recv_sems.at[mine],
+                recv_sem=recv_sems.at[place],
                 device_id=where,
                 device_id_type=MESH,
             )
 
         def start(d, carry):
-            copy(*peer(d)).start()
+            there, where = peer(d)
+            copy(there, where, mine).start()
             return carry
 
         def sent(d, carry):
-            copy(*peer(d)).wait_send()
+            there, where = peer(d)
+            copy(there, where, mine).wait_send()
             return carry
 
         def arrived(d, carry):
             there, where = peer(d)
-            pltpu.make_async_remote_copy(
-                src_ref=source.at[there],
-                dst_ref=landing.at[there],
-                send_sem=send_sems.at[there],
-                recv_sem=recv_sems.at[there],
-                device_id=where,
-                device_id_type=MESH,
-            ).wait_recv()
+            copy(there, where, there).wait_recv()
             return carry
 
         return (
@@ -196,16 +237,59 @@
             lambda: lax.fori_loop(1, count, sent, 0),
         )
 
-    start_a, arrived_a, sent_a = exchange(exp_id, n_exp, send_a, recv_a, me_e, sa_sem, ra_sem)
-    start_n, arrived_n, sent_n = exchange(near_id, NEAR, send_n, recv_n, me_near, sn_sem, rn_sem)
-    start_m, arrived_m, sent_m = exchange(near_id, NEAR, send_m, recv_m, me_near, sm_sem, rm_sem)
-    start_b, arrived_b, sent_b = exchange(exp_id, n_exp, send_b, recv_b, me_e, sb_sem, rb_sem)
-    start_r, arrived_r, sent_r = exchange(head_id, n_head, send_r, recv_r, me_x, sr_sem, rr_sem)
-    start_d, arrived_d, sent_d = exchange(
-        plane_id, n_plane, send_d, recv_d, me_plane, sd_sem, rd_sem
-    )
-    start_o, arrived_o, sent_o = exchange(
-        plane_id, n_plane, send_o, recv_o, me_plane, so_sem, ro_sem
+    def at(ref):
+        return lambda k: ref.at[k]
+
+    def whole(ref):
+        return lambda k: ref
+
+    def across(ref):
+        return lambda k: ref.at[:, k % CORES, k // CORES]
+
+    start_a, arrived_a, sent_a = exchange(
+        exp_id, n_exp, at(send_a), at(recv_a), me_e, sa_sem, ra_sem
+    )
+    start_n, arrived_n, sent_n = exchange(
+        near_id, NEAR, at(send_n), at(recv_n), me_near, sn_sem, rn_sem
+    )
+    start_m, arrived_m, sent_m = exchange(
+        near_id, NEAR, at(send_m), at(recv_m), me_near, sm_sem, rm_sem
+    )
+    start_b, arrived_b, sent_b = exchange(
+        exp_id, n_exp, at(send_b), at(recv_b), me_e, sb_sem, rb_sem
+    )
+    start_r, arrived_r, sent_r = exchange(
+        head_id, n_head, at(send_r), at(recv_r), me_x, sr_sem, rr_sem
+    )
+    start_tx, arrived_tx, sent_tx = exchange(
+        head_id, n_head, whole(table_x), at(tables_x), me_x, tx_send, tx_recv
+    )
+    start_ty, arrived_ty, sent_ty = exchange(
+        y_id, n_y, whole(table_y), at(tables_y), me_y, ty_send, ty_recv
+    )
+    start_gx, arrived_gx, sent_gx = exchange(
+        head_id, n_head, whole(half_x), at(gathered_x), me_x, gx_send, gx_recv
+    )
+    start_gy, arrived_gy, sent_gy = exchange(
+        y_id, n_y, whole(half_y), at(gathered_y), me_y, gy_send, gy_recv
+    )
+    start_lx, arrived_lx, sent_lx = exchange(
+        exp_id, n_exp, at(rows_x), at(landed_x), me_e, lx_send, lx_recv
+    )
+    start_ly, arrived_ly, sent_ly = exchange(
+        block_id, n_head * CORES, at(rows_y), across(landed_y), me_block, ly_send, ly_recv
+    )
+    start_bx, arrived_bx, sent_bx = exchange(
+        exp_id, n_exp, at(made_x), at(back_x), me_e, bx_send, bx_recv
+    )
+    start_by, arrived_by, sent_by = exchange(
+        block_id, n_head * CORES, across(made_y), at(back_y), me_block, by_send, by_recv
+    )
+    start_fx, arrived_fx, sent_fx = exchange(
+        head_id, n_head, at(sums_x), at(last_x), me_x, fx_send, fx_recv
+    )
+    start_fy, arrived_fy, sent_fy = exchange(
+        y_id, n_y, at(sums_y), at(last_y), me_y, fy_send, fy_recv
     )
 
     dt = dt_ref[...]
@@ -241,13 +325,45 @@
         ).astype(BF16)
         for k in range(per_send):
             send_a[g * per_send + k, 0:own_rows, :] = update[k * own_rows : (k + 1) * own_rows, :]
+    tile_row = iota((n_exp * 16, 2 * heads), 0)
+    its_head = tile_row // 16 * own_heads + tile_row % own_heads + heads * (tile_row % 16 // 8)
+    logs = dot(
+        jnp.where(its_head == iota((n_exp * 16, 2 * heads), 1), 1.0, 0.0).astype(BF16),
+        jnp.concatenate([total_high, total_low], axis=0),
+    ).astype(BF16)
     for k in range(n_exp):
-        send_a[k, own_rows : own_rows + heads, :] = total_high
-        send_a[k, own_rows + heads : own_rows + 2 * heads, :] = total_low
-
-    pl.semaphore_wait(barrier, (len(REACH) if n_far > 1 else 0) + (NEAR - 1) + (n_plane - 1))
+        send_a[k, own_rows : own_rows + 16, :] = logs[k * 16 : (k + 1) * 16]
+
+    expert_row = iota((n_plane, rows_here), 0)
+    routed = jnp.zeros((n_plane, rows_here), F32)
+    gate = jnp.zeros((n_plane, rows_here), F32)
+    for k in range(routes_ref.shape[0]):
+        hit = expert_row == routes_ref[k]
+        routed = jnp.where(hit, 1.0, routed)
+        gate = jnp.where(hit, gates_ref[k], gate)
+    upto_here = jnp.where(
+        iota((rows_here, rows_here), 0) <= iota((rows_here, rows_here), 1), 1.0, 0.0
+    ).astype(BF16)
+    place = routed * dot(routed.astype(BF16), upto_here)
+    gate_high, gate_low = halves(gate)
+    table = jnp.concatenate([place.astype(BF16), gate_high, gate_low], axis=0)
+
+    def in_lanes(count, mine):
+        lanes = (rows_here, count * rows_here)
+        spot = iota(lanes, 1) == iota(lanes, 0) + mine * rows_here
+        return dot(table, jnp.where(spot, 1.0, 0.0).astype(BF16)).astype(BF16)
+
+    table_x[...] = in_lanes(n_head, me_x)
+    table_y[...] = in_lanes(n_y, me_y)
+
+    far_peers = len(REACH) if n_far > 1 else 0
+    pl.semaphore_wait(barrier, far_peers + (NEAR - 1) + (n_exp - 1) + (n_head - 1) * CORES)
     start_a()
     recv_a[me_e] = send_a[me_e]
+    start_tx()
+    start_ty()
+    tables_x[me_x] = table_x[...]
+    tables_y[me_y] = table_y[...]
 
     first_half = iota((tokens, 2 * HEAD_DIM), 1) < HEAD_DIM
     skip_wide = dot(dskip_ref[...], spread, 1, 0, EXACT)
@@ -271,44 +387,17 @@
             y_ref[:, lanes] = inside + skip_wide[:, lanes] * pair.astype(F32)
     grow_ref[...] = dot(grow, spread, 1, 0, EXACT)
 
-    expert_row = iota((n_plane, rows_here), 0)
-    routed = jnp.zeros((n_plane, rows_here), F32)
-    gate = jnp.zeros((n_plane, rows_here), F32)
-    for k in range(routes_ref.shape[0]):
-        hit = expert_row == routes_ref[k]
-        routed = jnp.where(hit, 1.0, routed)
-        gate = jnp.where(hit, gates_ref[k], gate)
-    ahead = jnp.where(
-        iota((rows_here, rows_here), 0) < iota((rows_here, rows_here), 1), 1.0, 0.0
-    ).astype(BF16)
-    place = jnp.where(routed > 0.5, dot(routed.astype(BF16), ahead), -1.0)
-    slots = n_plane * ROOM
-    repeat = jnp.where(
-        iota((slots, n_plane), 0) // ROOM == iota((slots, n_plane), 1), 1.0, 0.0
-    ).astype(BF16)
-    place_wide = dot(repeat, place.astype(BF16))
-    chosen = place_wide == (iota((slots, rows_here), 0) % ROOM).astype(F32)
-    gate_high, gate_low = halves(gate)
-    pick = jnp.where(chosen, 1.0, 0.0).astype(BF16)
-    pick_high = jnp.where(chosen, dot(repeat, gate_high), 0.0).astype(BF16)
-    pick_low = jnp.where(chosen, dot(repeat, gate_low), 0.0).astype(BF16)
-
     arrived_a()
-    head_row = iota((heads, STATE), 0)
     own_row = iota((own_rows, STATE), 0)
     state = jnp.zeros((own_rows, STATE), F32)
     log_sum = jnp.zeros((own_rows, STATE), F32)
     for k in range(n_exp):
         pre_ref[k] = state
         lpre_ref[k] = log_sum
-        high = recv_a[k, own_rows : own_rows + heads, :].astype(F32)
-        low = recv_a[k, own_rows + heads : own_rows + 2 * heads, :].astype(F32)
-        both = high + low
+        tile = recv_a[k, own_rows : own_rows + 16, :].astype(F32)
         log_here = jnp.zeros((own_rows, STATE), F32)
         for h in range(own_heads):
-            one = jnp.sum(
-                jnp.where(head_row == me_e * own_heads + h, both, 0.0), axis=0, keepdims=True
-            )
+            one = tile[h : h + 1, :] + tile[8 + h : 9 + h, :]
             log_here = jnp.where(own_row // HEAD_DIM == h, one, log_here)
         state = jnp.exp(log_here) * state + recv_a[k, 0:own_rows, :].astype(F32)
         log_sum = log_sum + log_here
@@ -359,13 +448,57 @@
             device_id_type=MESH,
         )
 
+    def choose(tables, pick, expert, inner):
+        row, lane = iota(pick.shape[1:], 0), iota(pick.shape[1:], 1)
+        slots = pick.shape[1]
+        wanted = expert(iota((slots, n_plane), 0) // (inner * ROOM))
+        repeat = jnp.where(wanted == iota((slots, n_plane), 1), 1.0, 0.0).astype(BF16)
+        every = jnp.sum(tables[...].astype(F32), axis=0).astype(BF16)
+        spot = dot(repeat, every[0:n_plane])
+        chosen = (spot == (row % ROOM + 1).astype(F32)) & (
+            row // ROOM % inner == lane // rows_here
+        )
+        pick[0] = jnp.where(chosen, 1.0, 0.0).astype(BF16)
+        for part in (1, 2):
+            wide = dot(repeat, every[part * n_plane : (part + 1) * n_plane])
+            pick[part] = jnp.where(chosen, wide, 0.0).astype(BF16)
+
+    def choose_both():
+        arrived_tx()
+        arrived_ty()
+        choose(tables_x, pick_x, lambda k: me_x * n_exp + k, n_head)
+        choose(
+            tables_y,
+            pick_y,
+            lambda k: k // CORES * n_exp + me_y * CORES + k % CORES,
+            n_y,
+        )
+
+    if n_far == 1:
+        choose_both()
     if n_far > 1:
         put(0, part, part_log)
         copies = [far_copy(d, 0, slot) for slot, d in enumerate(REACH)]
-        for copy in copies:
-            copy.start()
-        for copy in copies[:3]:
-            copy.wait_recv()
+        copies += [far_copy(2, 1, 4), far_copy(-2, 2, 5)]
+        early = me_far <= 1
+        relays = early | (me_far == 7)
+        goes = (
+            me_far <= 6,
+            me_far <= 5,
+            me_far <= 2,
+            early,
+            (me_far >= 1) & (me_far <= 5),
+            relays,
+        )
+        comes = (me_far >= 1, me_far >= 2, relays, me_far >= 6, me_far >= 3, me_far >= 5)
+
+        def only(slots, flags, act):
+            for slot in slots:
+                pl.when(flags[slot])(functools.partial(act, copies[slot]))
+
+        only((1, 0, 3, 2), goes, lambda copy: copy.start())
+        choose_both()
+        only((0, 1, 2), comes, lambda copy: copy.wait_recv())
         one, one_log = unpacked(recv_f, 0)
         two, two_log = unpacked(recv_f, 1)
         two = jnp.where(me_far >= 2, two, 0.0)
@@ -373,15 +506,12 @@
         fold = jnp.where(me_far >= 1, jnp.exp(one_log) * two + one, 0.0)
         fold_log = jnp.where(me_far >= 1, one_log + two_log, 0.0)
         put(1, fold, fold_log)
-        copies.append(far_copy(2, 1, 4))
-        copies[4].start()
+        only((4,), goes, lambda copy: copy.start())
         back, back_log = unpacked(recv_f, 2)
         put(2, back, back_log)
-        copies.append(far_copy(-2, 2, 5))
-        copies[5].start()
-        for copy in copies[3:]:
-            copy.wait_recv()
-        for slot, least in ((2, 7), (3, 6), (5, 5), (4, 2), (1, 2), (0, 1)):
+        only((5,), goes, lambda copy: copy.start())
+        only((3, 4, 5), comes, lambda copy: copy.wait_recv())
+        for slot, least in ((2, 7), (3, 6), (5, 5), (4, 3), (1, 2), (0, 1)):
             values, log_here = unpacked(recv_f, slot)
             chain = jnp.where(me_far >= least, jnp.exp(log_here) * chain + values, chain)
 
@@ -421,29 +551,65 @@
     moe_in = (hidden * scale * gain_ref[...].reshape(1, -1)).astype(BF16)
 
     model = moe_in.shape[1]
-    send_d[...] = dot(pick, moe_in).astype(BF16).reshape(n_plane, ROOM, model)
-    start_d()
-    recv_d[me_plane] = send_d[me_plane]
-    arrived_d()
+    split = half_x.shape[1]
+    half_x[...] = moe_in[:, :split]
+    half_y[...] = moe_in[:, split:]
+    start_gx()
+    start_gy()
+    gathered_x[me_x] = half_x[...]
+    gathered_y[me_y] = half_y[...]
+    arrived_gx()
+    picked = dot(pick_x[0], gathered_x[...].reshape(n_head * rows_here, split))
+    rows_x[...] = picked.astype(BF16).reshape(rows_x.shape)
+    start_lx()
+    arrived_gy()
+    picked = dot(pick_y[0], gathered_y[...].reshape(n_y * rows_here, model - split))
+    rows_y[...] = picked.astype(BF16).reshape(rows_y.shape)
+    start_ly()
+    landed_x[me_e] = rows_x[me_e]
+    landed_y[:, me_c, me_x] = rows_y[me_block]
     w_copies[1].wait()
     w_copies[2].wait()
-    rows = recv_d[...].reshape(slots, model)
-    raised = jnp.maximum(dot(rows, wup[0], 1, 1), 0.0)
+    slots = n_plane * ROOM
+    arrived_lx()
+    raised = dot(landed_x[...].reshape(slots, split), wup[0, :, :split], 1, 1)
+    arrived_ly()
+    raised += dot(landed_y[...].reshape(slots, model - split), wup[0, :, split:], 1, 1)
+    raised = jnp.maximum(raised, 0.0)
     activated = (raised * raised).astype(BF16)
-    send_o[...] = dot(activated, wdown[0]).astype(BF16).reshape(n_plane, ROOM, model)
-    start_o()
-    recv_o[me_plane] = send_o[me_plane]
-    arrived_o()
-    returned = recv_o[...].reshape(slots, model)
-    moe_sum = dot(pick_high, returned, 0, 0) + dot(pick_low, returned, 0, 0)
-    out_ref[0] = (hidden + moe_sum).astype(BF16)
-
-    for sent in (sent_a, sent_n, sent_m, sent_b, sent_r, sent_d, sent_o):
+
+    made_x[...] = dot(activated, wdown[0, :, :split]).astype(BF16).reshape(made_x.shape)
+    start_bx()
+    made_y[...] = dot(activated, wdown[0, :, split:]).astype(BF16).reshape(made_y.shape)
+    start_by()
+    back_x[me_e] = made_x[me_e]
+    back_y[me_block] = made_y[:, me_c, me_x]
+    arrived_bx()
+    back = back_x[...].reshape(slots, split)
+    summed = dot(pick_x[1], back, 0, 0) + dot(pick_x[2], back, 0, 0)
+    sums_x[...] = summed.astype(BF16).reshape(sums_x.shape)
+    start_fx()
+    arrived_by()
+    back = back_y[...].reshape(slots, model - split)
+    summed = dot(pick_y[1], back, 0, 0) + dot(pick_y[2], back, 0, 0)
+    sums_y[...] = summed.astype(BF16).reshape(sums_y.shape)
+    start_fy()
+    last_x[me_x] = sums_x[me_x]
+    last_y[me_y] = sums_y[me_y]
+    arrived_fx()
+    moe_sum = jnp.sum(last_x[...].astype(F32), axis=0)
+    out_ref[0, :, :split] = (hidden[:, :split] + moe_sum).astype(BF16)
+    arrived_fy()
+    moe_sum = jnp.sum(last_y[...].astype(F32), axis=0)
+    out_ref[0, :, split:] = (hidden[:, split:] + moe_sum).astype(BF16)
+
+    for sent in (sent_a, sent_tx, sent_ty, sent_n, sent_m, sent_b, sent_r):
         sent()
+    for sent in (sent_gx, sent_gy, sent_lx, sent_ly, sent_bx, sent_by, sent_fx, sent_fy):
+        sent()
 
     if n_far > 1:
-        for copy in copies:
-            copy.wait_send()
+        only(range(6), goes, lambda copy: copy.wait_send())
 
 
 def per_device(
@@ -495,7 +661,7 @@
             dma((count,)),
         ]
 
-    scratch += pair(n_exp, own_rows + 2 * heads, STATE)
+    scratch += pair(n_exp, own_rows + 16, STATE)
     scratch += pair(NEAR, near_rows + 16, STATE)
     scratch += [
         pltpu.VMEM((NEAR, near_rows, STATE), F32),
@@ -508,8 +674,33 @@
     scratch += pair(NEAR, near_rows, STATE)
     scratch += pair(n_exp, own_rows, STATE)
     scratch += pair(n_head, rows_here, model)
-    scratch += pair(n_plane, ROOM, model)
-    scratch += pair(n_plane, ROOM, model)
+    n_y = n_exp // CORES
+    split = model // 256 * 128
+    rest = model - split
+    slots = n_plane * ROOM
+
+    def crossing(source, landing, count):
+        return [pltpu.VMEM(source, BF16), pltpu.VMEM(landing, BF16), dma((count,)), dma((count,))]
+
+    table = (3 * n_plane, n_head * rows_here)
+    scratch += crossing(table, (n_head, *table), n_head)
+    table = (3 * n_plane, n_y * rows_here)
+    scratch += crossing(table, (n_y, *table), n_y)
+    scratch += [
+        pltpu.VMEM((3, slots, n_head * rows_here), BF16),
+        pltpu.VMEM((3, slots, n_y * rows_here), BF16),
+    ]
+    scratch += crossing((rows_here, split), (n_head, rows_here, split), n_head)
+    scratch += crossing((rows_here, rest), (n_y, rows_here, rest), n_y)
+    by_exp = (n_exp, n_head, ROOM, split)
+    by_block = (n_head * CORES, n_y, ROOM, rest)
+    by_source = (n_y, CORES, n_head, ROOM, rest)
+    scratch += crossing(by_exp, by_exp, n_exp)
+    scratch += crossing(by_block, by_source, n_head * CORES)
+    scratch += crossing(by_exp, by_exp, n_exp)
+    scratch += crossing(by_source, by_block, n_head * CORES)
+    scratch += pair(n_head, rows_here, split)
+    scratch += pair(n_y, rows_here, rest)
     return pl.pallas_call(
         functools.partial(kernel, sizes),
         out_shape=jax.ShapeDtypeStruct(resid.shape, BF16),

time: 119 us -> 94.9 us (0.80)
  the two profiles are of different devices: /device:TPU:25 before, /device:TPU:1 now
where the time goes in v3:
time: 94.9 us; the launch traced here: 94.7 us
  Pallas kernels  93.2 us (98%)
  local copies, waits for them, and re-layouts  1.54 us (2%)
    pallas_call x1, Pallas kernels, per_device(): pl.pallas_call(functools.partial(kernel, sizes), out_shape=jax.ShapeDtype...  93.2 us

profile of v3, /device:TPU:1, one launch (start us, length us, event | category | flops | bytes accessed | tf_op | source)
XLA Modules:
  0.0 94.7 jit_solution(15057209554359040455)
XLA Ops:
  0.0 93.2 %shard_map.145 = bf16[1,32,1344]{2,1,0:T(8,128)(2,1)} custom-call(bf16[128,1024]{1,0:T(8,128)(2,1)} %x_ref.1, bf16[128,1024]{1,0:T(8,128)(2,1)} %z_ref.1, bf16[128,256]{1,0:T(8,128)(2,1)} %b_ref.1, bf16[128,256]{1,0:T(8,128)(2,1)} %c_ref.1, f32[16,128]{1,0:T(8,128)} %bitcast.10, f32[1,16]{1,0:T(1,128)} %bitcast.14, f32[1,16]{1,0:T(1,128)} %bitcast.15, ...), custom_call_target="tpu_custom_call" | custom-call | tf_op jit(solution)/shard_map/pallas_call | solution.py:704
  93.2 1.5 %copy.17 = bf16[1,32,1344]{2,1,0:T(8,128)(2,1)} copy(bf16[1,32,1344]{2,1,0:T(8,128)(2,1)} %shard_map.145) | data formatting | bytes 172032

commit v4 on v3

--- a/solution.py
+++ b/solution.py
@@ -12,9 +12,12 @@
 ROOM = 16
 CORES = 2
 NEAR = 4
+OWN = {1: (0, 2, 4, 5, 6), 2: (4, 5), 3: (3, 4), 4: (3,), 5: (2,)}
+UPTO = {1: (1, 3), 2: (1, 3), 6: (1,)}
+RELAY = (7, 2)
+LANDS = ((1,), (2, 3, 7), (3, 6, 7), (4, 5, 6, 7), (5, 6, 7), (6, 7), (7,))
 F32 = jnp.float32
 BF16 = jnp.bfloat16
-REACH = (1, 2, -1, -2)
 MESH = pl.DeviceIdType.MESH
 EXACT = lax.Precision.HIGHEST
 
@@ -132,7 +135,6 @@
 ):
     n_seq, n_head, n_exp = sizes
     n_far = n_seq // NEAR
-    assert n_far in (1, 8)
     n_plane = n_head * n_exp
     tokens = x_ref.shape[0]
     heads = dt_ref.shape[0]
@@ -183,8 +185,7 @@
         return there, {"seq": me_far * NEAR + there}
 
     def far_id(d):
-        there = lax.rem(me_far + d + n_far, n_far)
-        return {"seq": there * NEAR + me_near}
+        return {"seq": (me_far + d) * NEAR + me_near}
 
     barrier = pltpu.get_barrier_semaphore()
 
@@ -195,9 +196,25 @@
 
         lax.fori_loop(1, count, one, 0)
 
+    def member(set_of):
+        found = me_far < 0
+        for group in set_of:
+            found = found | (me_far == group)
+        return found
+
+    def greet_far(d):
+        pl.semaphore_signal(barrier, inc=1, device_id=far_id(d), device_id_type=MESH)
+
+    far_peers = 0
     if n_far > 1:
-        for d in REACH:
-            pl.semaphore_signal(barrier, inc=1, device_id=far_id(d), device_id_type=MESH)
+        assert n_far == len(LANDS) + 1
+        for d in range(1, n_far):
+            low = set(OWN.get(d, ())) | set(UPTO.get(d, ()))
+            for there, ends in ((d, low), (-d, {group + d for group in low})):
+                if ends:
+                    meets = member(sorted(ends))
+                    pl.when(meets)(functools.partial(greet_far, there))
+                    far_peers = far_peers + jnp.where(meets, 1, 0)
     greet(near_id, NEAR)
     greet(exp_id, n_exp)
     for d in range(1, n_head):
@@ -356,7 +373,6 @@
     table_x[...] = in_lanes(n_head, me_x)
     table_y[...] = in_lanes(n_y, me_y)
 
-    far_peers = len(REACH) if n_far > 1 else 0
     pl.semaphore_wait(barrier, far_peers + (NEAR - 1) + (n_exp - 1) + (n_head - 1) * CORES)
     start_a()
     recv_a[me_e] = send_a[me_e]
@@ -431,22 +447,22 @@
         values, log_here = unpacked(recv_n, k)
         part = jnp.exp(log_here) * part + values
         part_log = part_log + log_here
-    chain = jnp.zeros((near_rows, STATE), F32)
-
-    def put(slot, values, logs):
-        values, tile = packed(values, logs)
-        send_f[slot, 0:near_rows, :] = values
-        send_f[slot, near_rows : near_rows + 16, :] = tile
-
-    def far_copy(d, source, slot):
+    def far_copy(d, source, slot, sem):
         return pltpu.make_async_remote_copy(
             src_ref=send_f.at[source],
             dst_ref=recv_f.at[slot],
-            send_sem=sf_sem.at[slot],
+            send_sem=sf_sem.at[sem],
             recv_sem=rf_sem.at[slot],
             device_id=far_id(d),
             device_id_type=MESH,
         )
+
+    def put(slot, values, tile):
+        send_f[slot, 0:near_rows, :] = values.astype(BF16)
+        send_f[slot, near_rows : near_rows + 16, :] = tile
+
+    final = jnp.full((16, STATE), -16384.0, BF16)
+    far_sends = []
 
     def choose(tables, pick, expert, inner):
         row, lane = iota(pick.shape[1:], 0), iota(pick.shape[1:], 1)
@@ -474,46 +490,26 @@
             n_y,
         )
 
-    if n_far == 1:
-        choose_both()
+    chain = jnp.zeros((near_rows, STATE), F32)
     if n_far > 1:
-        put(0, part, part_log)
-        copies = [far_copy(d, 0, slot) for slot, d in enumerate(REACH)]
-        copies += [far_copy(2, 1, 4), far_copy(-2, 2, 5)]
-        early = me_far <= 1
-        relays = early | (me_far == 7)
-        goes = (
-            me_far <= 6,
-            me_far <= 5,
-            me_far <= 2,
-            early,
-            (me_far >= 1) & (me_far <= 5),
-            relays,
-        )
-        comes = (me_far >= 1, me_far >= 2, relays, me_far >= 6, me_far >= 3, me_far >= 5)
-
-        def only(slots, flags, act):
-            for slot in slots:
-                pl.when(flags[slot])(functools.partial(act, copies[slot]))
-
-        only((1, 0, 3, 2), goes, lambda copy: copy.start())
-        choose_both()
-        only((0, 1, 2), comes, lambda copy: copy.wait_recv())
-        one, one_log = unpacked(recv_f, 0)
-        two, two_log = unpacked(recv_f, 1)
-        two = jnp.where(me_far >= 2, two, 0.0)
-        two_log = jnp.where(me_far >= 2, two_log, 0.0)
-        fold = jnp.where(me_far >= 1, jnp.exp(one_log) * two + one, 0.0)
-        fold_log = jnp.where(me_far >= 1, one_log + two_log, 0.0)
-        put(1, fold, fold_log)
-        only((4,), goes, lambda copy: copy.start())
-        back, back_log = unpacked(recv_f, 2)
-        put(2, back, back_log)
-        only((5,), goes, lambda copy: copy.start())
-        only((3, 4, 5), comes, lambda copy: copy.wait_recv())
-        for slot, least in ((2, 7), (3, 6), (5, 5), (4, 3), (1, 2), (0, 1)):
-            values, log_here = unpacked(recv_f, slot)
-            chain = jnp.where(me_far >= least, jnp.exp(log_here) * chain + values, chain)
+        put(0, *packed(part, part_log))
+        for d in sorted(OWN, reverse=True):
+            far_sends.append((member(OWN[d]), far_copy(d, 0, me_far, d)))
+            pl.when(far_sends[-1][0])(far_sends[-1][1].start)
+    choose_both()
+    if n_far > 1:
+        for k, group in enumerate(LANDS):
+            pl.when(member(group))(far_copy(0, 0, k, 0).wait_recv)
+            values, log_here = unpacked(recv_f, k)
+            chain = jnp.where(member(group), jnp.exp(log_here) * chain + values, chain)
+            if k == RELAY[1]:
+                put(2, chain, final)
+                far_sends.append((me_far == RELAY[0], far_copy(-1, 2, k, 0)))
+                pl.when(far_sends[-1][0])(far_sends[-1][1].start)
+        put(1, jnp.exp(part_log) * chain + part, final)
+        for d in sorted(UPTO, reverse=True):
+            far_sends.append((member(UPTO[d]), far_copy(d, 1, me_far, n_far + d)))
+            pl.when(far_sends[-1][0])(far_sends[-1][1].start)
 
     for k in range(NEAR):
         send_m[k] = (jnp.exp(lpn_ref[k, 0:1, :]) * chain + pn_ref[k]).astype(BF16)
@@ -608,8 +604,8 @@
     for sent in (sent_gx, sent_gy, sent_lx, sent_ly, sent_bx, sent_by, sent_fx, sent_fy):
         sent()
 
-    if n_far > 1:
-        only(range(6), goes, lambda copy: copy.wait_send())
+    for went, copy in far_sends:
+        pl.when(went)(copy.wait_send)
 
 
 def per_device(
@@ -631,7 +627,7 @@
     w_down,
 ):
     n_seq, n_head, n_exp = sizes
-    n_plane = n_head * n_exp
+    n_far, n_plane = n_seq // NEAR, n_head * n_exp
     tokens, heads = dt_in.shape
     channels = heads * HEAD_DIM
     own_rows = channels // n_exp
@@ -667,9 +663,9 @@
         pltpu.VMEM((NEAR, near_rows, STATE), F32),
         pltpu.VMEM((NEAR, 8, STATE), F32),
         pltpu.VMEM((3, near_rows + 16, STATE), BF16),
-        pltpu.VMEM((6, near_rows + 16, STATE), BF16),
-        dma((6,)),
-        dma((6,)),
+        pltpu.VMEM((n_far, near_rows + 16, STATE), BF16),
+        dma((2 * n_far,)),
+        dma((n_far,)),
     ]
     scratch += pair(NEAR, near_rows, STATE)
     scratch += pair(n_exp, own_rows, STATE)

time: 94.9 us -> 91 us (0.959)
  the two profiles are of different devices: /device:TPU:1 before, /device:TPU:993 now
where the time goes in v4:
time: 91 us; the launch traced here: 90.8 us
  Pallas kernels  89.2 us (98%)
  local copies, waits for them, and re-layouts  1.54 us (2%)
    pallas_call x1, Pallas kernels, per_device(): pl.pallas_call(functools.partial(kernel, sizes), out_shape=jax.ShapeDtype...  89.2 us

profile of v4, /device:TPU:993, one launch (start us, length us, event | category | flops | bytes accessed | tf_op | source)
XLA Modules:
  0.0 90.8 jit_solution(2819677711862211010)
XLA Ops:
  0.0 89.2 %shard_map.145 = bf16[1,32,1344]{2,1,0:T(8,128)(2,1)} custom-call(bf16[128,1024]{1,0:T(8,128)(2,1)} %x_ref.1, bf16[128,1024]{1,0:T(8,128)(2,1)} %z_ref.1, bf16[128,256]{1,0:T(8,128)(2,1)} %b_ref.1, bf16[128,256]{1,0:T(8,128)(2,1)} %c_ref.1, f32[16,128]{1,0:T(8,128)} %bitcast.10, f32[1,16]{1,0:T(1,128)} %bitcast.14, f32[1,16]{1,0:T(1,128)} %bitcast.15, ...), custom_call_target="tpu_custom_call" | custom-call | tf_op jit(solution)/shard_map/pallas_call | solution.py:700
  89.2 1.5 %copy.17 = bf16[1,32,1344]{2,1,0:T(8,128)(2,1)} copy(bf16[1,32,1344]{2,1,0:T(8,128)(2,1)} %shard_map.145) | data formatting | bytes 172032

commit v5 on v4

--- a/solution.py
+++ b/solution.py
@@ -12,10 +12,11 @@
 ROOM = 16
 CORES = 2
 NEAR = 4
-OWN = {1: (0, 2, 4, 5, 6), 2: (4, 5), 3: (3, 4), 4: (3,), 5: (2,)}
-UPTO = {1: (1, 3), 2: (1, 3), 6: (1,)}
-RELAY = (7, 2)
-LANDS = ((1,), (2, 3, 7), (3, 6, 7), (4, 5, 6, 7), (5, 6, 7), (6, 7), (7,))
+OWN = {1: (0, 2, 3, 4, 5, 6), 2: (4, 5), 3: (4,)}
+UPTO = {1: (1, 3), 2: (1,), 6: (1,)}
+RELAY = (7, 1, (-1, -2))
+LANDS = ((1,), (2, 3, 5, 6, 7), (3,), (4,), (5, 6, 7), (6, 7), (7,))
+RUN = 7
 F32 = jnp.float32
 BF16 = jnp.bfloat16
 MESH = pl.DeviceIdType.MESH
@@ -90,6 +91,10 @@
     recv_r,
     sr_sem,
     rr_sem,
+    send_q,
+    recv_q,
+    sq_sem,
+    rq_sem,
     table_x,
     tables_x,
     tx_send,
@@ -100,6 +105,8 @@
     ty_recv,
     pick_x,
     pick_y,
+    gates_x,
+    gates_y,
     half_x,
     gathered_x,
     gx_send,
@@ -233,8 +240,8 @@
                 device_id_type=MESH,
             )
 
-        def start(d, carry):
-            there, where = peer(d)
+        def start(k, carry):
+            there, where = peer(1 + lax.rem(k + count // 2 - 2, count - 1))
             copy(there, where, mine).start()
             return carry
 
@@ -277,6 +284,9 @@
     )
     start_r, arrived_r, sent_r = exchange(
         head_id, n_head, at(send_r), at(recv_r), me_x, sr_sem, rr_sem
+    )
+    start_q, arrived_q, sent_q = exchange(
+        head_id, n_head, at(send_q), at(recv_q), me_x, sq_sem, rq_sem
     )
     start_tx, arrived_tx, sent_tx = exchange(
         head_id, n_head, whole(table_x), at(tables_x), me_x, tx_send, tx_recv
@@ -351,6 +361,10 @@
     for k in range(n_exp):
         send_a[k, own_rows : own_rows + 16, :] = logs[k * 16 : (k + 1) * 16]
 
+    pl.semaphore_wait(barrier, far_peers + (NEAR - 1) + (n_exp - 1) + (n_head - 1) * CORES)
+    start_a()
+    recv_a[me_e] = send_a[me_e]
+
     expert_row = iota((n_plane, rows_here), 0)
     routed = jnp.zeros((n_plane, rows_here), F32)
     gate = jnp.zeros((n_plane, rows_here), F32)
@@ -372,10 +386,6 @@
 
     table_x[...] = in_lanes(n_head, me_x)
     table_y[...] = in_lanes(n_y, me_y)
-
-    pl.semaphore_wait(barrier, far_peers + (NEAR - 1) + (n_exp - 1) + (n_head - 1) * CORES)
-    start_a()
-    recv_a[me_e] = send_a[me_e]
     start_tx()
     start_ty()
     tables_x[me_x] = table_x[...]
@@ -464,9 +474,9 @@
     final = jnp.full((16, STATE), -16384.0, BF16)
     far_sends = []
 
-    def choose(tables, pick, expert, inner):
-        row, lane = iota(pick.shape[1:], 0), iota(pick.shape[1:], 1)
-        slots = pick.shape[1]
+    def choose(tables, pick, gate_pick, expert, inner):
+        row, lane = iota(pick.shape, 0), iota(pick.shape, 1)
+        slots = pick.shape[0]
         wanted = expert(iota((slots, n_plane), 0) // (inner * ROOM))
         repeat = jnp.where(wanted == iota((slots, n_plane), 1), 1.0, 0.0).astype(BF16)
         every = jnp.sum(tables[...].astype(F32), axis=0).astype(BF16)
@@ -474,38 +484,49 @@
         chosen = (spot == (row % ROOM + 1).astype(F32)) & (
             row // ROOM % inner == lane // rows_here
         )
-        pick[0] = jnp.where(chosen, 1.0, 0.0).astype(BF16)
+        pick[...] = jnp.where(chosen, 1.0, 0.0).astype(BF16)
         for part in (1, 2):
             wide = dot(repeat, every[part * n_plane : (part + 1) * n_plane])
-            pick[part] = jnp.where(chosen, wide, 0.0).astype(BF16)
+            gate_pick[part - 1] = jnp.where(chosen, wide, 0.0).T.astype(BF16)
 
     def choose_both():
         arrived_tx()
         arrived_ty()
-        choose(tables_x, pick_x, lambda k: me_x * n_exp + k, n_head)
+        choose(tables_x, pick_x, gates_x, lambda k: me_x * n_exp + k, n_head)
         choose(
             tables_y,
             pick_y,
+            gates_y,
             lambda k: k // CORES * n_exp + me_y * CORES + k % CORES,
             n_y,
         )
 
     chain = jnp.zeros((near_rows, STATE), F32)
     if n_far > 1:
-        put(0, *packed(part, part_log))
+        for group, slot in ((3, 2), (4, RUN)):
+            pl.when(me_far == group)(far_copy(0, 0, slot, 0).wait_recv)
+        run, run_log = part, part_log
+        for group, slot in ((3, 2), (4, RUN)):
+            values, log_here = unpacked(recv_f, slot)
+            run = jnp.where(me_far == group, jnp.exp(part_log) * values + part, run)
+            run_log = jnp.where(me_far == group, log_here + part_log, run_log)
+        put(0, *packed(run, run_log))
         for d in sorted(OWN, reverse=True):
-            far_sends.append((member(OWN[d]), far_copy(d, 0, me_far, d)))
+            slot = jnp.where(me_far == 3, RUN, me_far)
+            far_sends.append((member(OWN[d]), far_copy(d, 0, slot, d)))
             pl.when(far_sends[-1][0])(far_sends[-1][1].start)
     choose_both()
     if n_far > 1:
         for k, group in enumerate(LANDS):
-            pl.when(member(group))(far_copy(0, 0, k, 0).wait_recv)
+            if k != 2:
+                pl.when(member(group))(far_copy(0, 0, k, 0).wait_recv)
             values, log_here = unpacked(recv_f, k)
             chain = jnp.where(member(group), jnp.exp(log_here) * chain + values, chain)
             if k == RELAY[1]:
                 put(2, chain, final)
-                far_sends.append((me_far == RELAY[0], far_copy(-1, 2, k, 0)))
-                pl.when(far_sends[-1][0])(far_sends[-1][1].start)
+                for sem, d in zip((0, n_far - 1), RELAY[2]):
+                    far_sends.append((me_far == RELAY[0], far_copy(d, 2, k, sem)))
+                    pl.when(far_sends[-1][0])(far_sends[-1][1].start)
         put(1, jnp.exp(part_log) * chain + part, final)
         for d in sorted(UPTO, reverse=True):
             far_sends.append((member(UPTO[d]), far_copy(d, 1, me_far, n_far + d)))
@@ -535,19 +556,23 @@
         normed.append((gated * inverse * normw_ref[:, lanes]).astype(BF16))
     normed = jnp.concatenate(normed, axis=1)
     w_copies[0].wait()
-    projected = dot(normed, wout[...], 1, 1).astype(BF16)
-    for k in range(n_head):
-        send_r[k] = projected[k * rows_here : (k + 1) * rows_here]
-    start_r()
+    split = half_x.shape[1]
+    for send, rows, start in ((send_r, wout[:split], start_r), (send_q, wout[split:], start_q)):
+        projected = dot(normed, rows, 1, 1).astype(BF16)
+        for k in range(n_head):
+            send[k] = projected[k * rows_here : (k + 1) * rows_here]
+        start()
     recv_r[me_x] = send_r[me_x]
+    recv_q[me_x] = send_q[me_x]
     arrived_r()
     mixed = jnp.sum(recv_r[...].astype(F32), axis=0)
+    arrived_q()
+    mixed = jnp.concatenate([mixed, jnp.sum(recv_q[...].astype(F32), axis=0)], axis=1)
     hidden = (resid_ref[0].astype(F32) + mixed).astype(BF16).astype(F32)
     scale = lax.rsqrt(jnp.mean(hidden * hidden, axis=1, keepdims=True) + 1e-05)
     moe_in = (hidden * scale * gain_ref[...].reshape(1, -1)).astype(BF16)
 
     model = moe_in.shape[1]
-    split = half_x.shape[1]
     half_x[...] = moe_in[:, :split]
     half_y[...] = moe_in[:, split:]
     start_gx()
@@ -555,11 +580,11 @@
     gathered_x[me_x] = half_x[...]
     gathered_y[me_y] = half_y[...]
     arrived_gx()
-    picked = dot(pick_x[0], gathered_x[...].reshape(n_head * rows_here, split))
+    picked = dot(pick_x[...], gathered_x[...].reshape(n_head * rows_here, split))
     rows_x[...] = picked.astype(BF16).reshape(rows_x.shape)
     start_lx()
     arrived_gy()
-    picked = dot(pick_y[0], gathered_y[...].reshape(n_y * rows_here, model - split))
+    picked = dot(pick_y[...], gathered_y[...].reshape(n_y * rows_here, model - split))
     rows_y[...] = picked.astype(BF16).reshape(rows_y.shape)
     start_ly()
     landed_x[me_e] = rows_x[me_e]
@@ -582,12 +607,12 @@
     back_y[me_block] = made_y[:, me_c, me_x]
     arrived_bx()
     back = back_x[...].reshape(slots, split)
-    summed = dot(pick_x[1], back, 0, 0) + dot(pick_x[2], back, 0, 0)
+    summed = dot(gates_x[0], back) + dot(gates_x[1], back)
     sums_x[...] = summed.astype(BF16).reshape(sums_x.shape)
     start_fx()
     arrived_by()
     back = back_y[...].reshape(slots, model - split)
-    summed = dot(pick_y[1], back, 0, 0) + dot(pick_y[2], back, 0, 0)
+    summed = dot(gates_y[0], back) + dot(gates_y[1], back)
     sums_y[...] = summed.astype(BF16).reshape(sums_y.shape)
     start_fy()
     last_x[me_x] = sums_x[me_x]
@@ -599,7 +624,7 @@
     moe_sum = jnp.sum(last_y[...].astype(F32), axis=0)
     out_ref[0, :, split:] = (hidden[:, split:] + moe_sum).astype(BF16)
 
-    for sent in (sent_a, sent_tx, sent_ty, sent_n, sent_m, sent_b, sent_r):
+    for sent in (sent_a, sent_tx, sent_ty, sent_n, sent_m, sent_b, sent_r, sent_q):
         sent()
     for sent in (sent_gx, sent_gy, sent_lx, sent_ly, sent_bx, sent_by, sent_fx, sent_fy):
         sent()
@@ -669,10 +694,11 @@
     ]
     scratch += pair(NEAR, near_rows, STATE)
     scratch += pair(n_exp, own_rows, STATE)
-    scratch += pair(n_head, rows_here, model)
     n_y = n_exp // CORES
     split = model // 256 * 128
     rest = model - split
+    scratch += pair(n_head, rows_here, split)
+    scratch += pair(n_head, rows_here, rest)
     slots = n_plane * ROOM
 
     def crossing(source, landing, count):
@@ -683,8 +709,10 @@
     table = (3 * n_plane, n_y * rows_here)
     scratch += crossing(table, (n_y, *table), n_y)
     scratch += [
-        pltpu.VMEM((3, slots, n_head * rows_here), BF16),
-        pltpu.VMEM((3, slots, n_y * rows_here), BF16),
+        pltpu.VMEM((slots, n_head * rows_here), BF16),
+        pltpu.VMEM((slots, n_y * rows_here), BF16),
+        pltpu.VMEM((2, n_head * rows_here, slots), BF16),
+        pltpu.VMEM((2, n_y * rows_here, slots), BF16),
     ]
     scratch += crossing((rows_here, split), (n_head, rows_here, split), n_head)
     scratch += crossing((rows_here, rest), (n_y, rows_here, rest), n_y)

time: 91 us -> 90.4 us (level)
  the two profiles are of different devices: /device:TPU:993 before, /device:TPU:992 now
where the time goes in v5:
time: 90.4 us; the launch traced here: 90.2 us
  Pallas kernels  88.7 us (98%)
  local copies, waits for them, and re-layouts  1.54 us (2%)
    pallas_call x1, Pallas kernels, per_device(): pl.pallas_call(functools.partial(kernel, sizes), out_shape=jax.ShapeDtype...  88.7 us

profile of v5, /device:TPU:992, one launch (start us, length us, event | category | flops | bytes accessed | tf_op | source)
XLA Modules:
  0.0 90.2 jit_solution(15696459075908807873)
XLA Ops:
  0.0 88.7 %shard_map.145 = bf16[1,32,1344]{2,1,0:T(8,128)(2,1)} custom-call(bf16[128,1024]{1,0:T(8,128)(2,1)} %x_ref.1, bf16[128,1024]{1,0:T(8,128)(2,1)} %z_ref.1, bf16[128,256]{1,0:T(8,128)(2,1)} %b_ref.1, bf16[128,256]{1,0:T(8,128)(2,1)} %c_ref.1, f32[16,128]{1,0:T(8,128)} %bitcast.10, f32[1,16]{1,0:T(1,128)} %bitcast.14, f32[1,16]{1,0:T(1,128)} %bitcast.15, ...), custom_call_target="tpu_custom_call" | custom-call | tf_op jit(solution)/shard_map/pallas_call | solution.py:728
  88.7 1.5 %copy.17 = bf16[1,32,1344]{2,1,0:T(8,128)(2,1)} copy(bf16[1,32,1344]{2,1,0:T(8,128)(2,1)} %shard_map.145) | data formatting | bytes 172032
